TPU v7x, 128 devices: a whole 4x4x4 slice. The times are simulated.
128 devices in a mesh: expert: 16 (over z, y), tensor: 8 (over x, core).
Axes of the slice: x: 4, y: 4, z: 4, core: 2. Of those that a mesh axis runs over, the one named last changes fastest.
Arguments:
- tokens: bfloat16 [2048, 8192], P('expert', 'tensor'), may hold values from -25 to 25, as said below
- routes: int32 [2048, 2], P('expert'), may hold values from 0 to 15, all different within a row; in each aligned block of 128 rows (0 to 127, 128 to 255, ...) at most 24 rows name the same one
- norm_gain: float32 [2, 8192], P(None, 'tensor'), may hold values from 0.5 to 1.5
- router_weight: bfloat16 [2, 8192, 16], P(None, 'tensor'), may hold values from -0.0625 to 0.0625
- gate_codes: int32 [2, 16, 4096, 1024], P(None, 'expert', None, 'tensor'), may hold values from 0 to 255
- gate_scales: int32 [2, 16, 64, 1024], P(None, 'expert', None, 'tensor'), may hold values from 8 to 10
- up_codes: int32 [2, 16, 4096, 1024], P(None, 'expert', None, 'tensor'), may hold values from 0 to 255
- up_scales: int32 [2, 16, 64, 1024], P(None, 'expert', None, 'tensor'), may hold values from 8 to 10
- down_codes: int32 [2, 16, 512, 8192], P(None, 'expert', 'tensor'), may hold values from 0 to 255
- down_scales: int32 [2, 16, 8, 8192], P(None, 'expert', 'tensor'), may hold values from 6 to 8
Outputs:
- hidden_out: bfloat16 [2048, 8192], P('expert', 'tensor')
Inputs may be any that keep to these rules, and one draw needn't show every extreme that they name: `routes`: in the rows of one index of expert (128 aligned rows) no expert is named by more than 24 rows, a bound that some block reaches; the two experts of a row differ. `tokens`: token activations.
All inputs are finite; a program needn't handle non-finite values.
Results may differ from a plain program's by a relative error of at most 0.029.
Values may be sent and summed in bfloat16 or wider, within the bound.
A program may use at most 192 MiB of HBM per device.

v0:
```python
import math

import jax
import jax.numpy as jnp
import numpy as np
from jax import lax
from jax.sharding import PartitionSpec as P

LAYERS = 2


def from_partner(shard, axis, stride):
    return lax.ppermute(shard, axis, [(i, i ^ 1 << stride) for i in range(lax.axis_size(axis))])


def hadamard(table_order):
    matrix = np.ones((1, 1), np.float32)
    for repeat_idx in range(table_order.bit_length() - 1):
        matrix = np.kron(np.array([[1.0, 1.0], [1.0, -1.0]], np.float32), matrix)
    return matrix


def unpack(words):
    shifts = jnp.arange(2, dtype=jnp.int32) * 4
    nibbles = jnp.bitwise_and(jnp.right_shift(words[:, None, :], shifts[None, :, None]), 15) - 8
    return nibbles.reshape(words.shape[0] * 2, words.shape[1])


def dequant(words, scales):
    codes = unpack(words)
    groups = scales.shape[0]
    shaped = codes.reshape(groups, codes.shape[0] // groups, codes.shape[1]).astype(jnp.float32)
    factor = jnp.exp2(-scales.astype(jnp.float32))
    return (shaped * factor[:, None, :]).reshape(codes.shape).astype(jnp.bfloat16)


def rotate_local(matrix_rows, first_table, second_table):
    row_count = matrix_rows.shape[0]
    first_order = first_table.shape[0]
    second_order = second_table.shape[0]
    shaped = matrix_rows.reshape(row_count, first_order, second_order)
    section_one = jnp.einsum(
        "rab,bc->rac", shaped, second_table, preferred_element_type=jnp.float32
    )
    section_two = jnp.einsum(
        "rac,ad->rdc", section_one, first_table, precision=lax.Precision.HIGHEST
    )
    return section_two.reshape(row_count, first_order * second_order)


def rotate_butterfly(normed, first_table, second_table, parts_count):
    partial_value = rotate_local(normed, first_table, second_table)
    tensor_index = lax.axis_index("tensor")
    for bit_pos in range(parts_count.bit_length() - 1):
        partner = from_partner(partial_value.astype(jnp.bfloat16), "tensor", bit_pos).astype(
            partial_value.dtype
        )
        upper = tensor_index >> bit_pos & 1 == 1
        partial_value = jnp.where(upper, partner - partial_value, partial_value + partner)
    full_width = parts_count * normed.shape[1]
    return (partial_value * (1.0 / math.sqrt(full_width))).astype(jnp.bfloat16)


def expert_activation(inputs, gate_w, up_w):
    gate_out = jnp.dot(inputs, gate_w, preferred_element_type=jnp.float32)
    up_out = jnp.dot(inputs, up_w, preferred_element_type=jnp.float32)
    return (jax.nn.silu(gate_out) * up_out).astype(jnp.bfloat16)


def per_device(
    tokens,
    routes,
    norm_gain,
    router_weight,
    gate_codes,
    gate_scales,
    up_codes,
    up_scales,
    down_codes,
    down_scales,
):
    parts_count = lax.axis_size("tensor")
    expert_count = lax.axis_size("expert")
    tok_count = tokens.shape[0]
    local_width = tokens.shape[1]
    full_width = local_width * parts_count
    capacity = 3 * tok_count // expert_count
    slot_total = expert_count * capacity
    first_order = 1 << (local_width.bit_length() - 1) // 2
    second_order = local_width // first_order
    first_table = jnp.asarray(hadamard(first_order), jnp.float32)
    second_table = jnp.asarray(hadamard(second_order), jnp.bfloat16)
    flat_routes = routes.reshape(-1)
    expert_ids = jnp.arange(expert_count, dtype=jnp.int32)
    onehot = (flat_routes[:, None] == expert_ids[None, :]).astype(jnp.int32)
    earlier = jnp.cumsum(onehot, axis=0) - onehot
    ranks = jnp.sum(earlier * onehot, axis=1)
    slot_ids = flat_routes * capacity + ranks
    token_of = jnp.arange(2 * tok_count, dtype=jnp.int32) // 2
    matches = (slot_ids[None, :] == jnp.arange(slot_total, dtype=jnp.int32)[:, None]).astype(
        jnp.int32
    )
    slot_token = jnp.sum(matches * token_of[None, :], axis=1)
    slot_valid = jnp.sum(matches, axis=1) > 0
    first_slot = slot_ids[0::2]
    second_slot = slot_ids[1::2]
    first_pick = (routes[:, 0:1] == expert_ids[None, :]).astype(jnp.float32)
    second_pick = (routes[:, 1:2] == expert_ids[None, :]).astype(jnp.float32)
    stream = tokens.astype(jnp.float32)
    for layer_idx in range(LAYERS):
        square = lax.psum(jnp.sum(stream * stream, axis=1), "tensor")
        normed = (
            stream * lax.rsqrt(square / full_width + 1e-05)[:, None] * norm_gain[layer_idx][None, :]
        ).astype(jnp.bfloat16)
        logits = lax.psum(
            jnp.dot(normed, router_weight[layer_idx], preferred_element_type=jnp.float32), "tensor"
        )
        first_logit = jnp.sum(logits * first_pick, axis=1)
        second_logit = jnp.sum(logits * second_pick, axis=1)
        first_weight = jax.nn.sigmoid(first_logit - second_logit)
        moving = rotate_butterfly(normed, first_table, second_table, parts_count)
        gate_w = dequant(gate_codes[layer_idx, 0], gate_scales[layer_idx, 0])
        up_w = dequant(up_codes[layer_idx, 0], up_scales[layer_idx, 0])
        down_w = dequant(down_codes[layer_idx, 0], down_scales[layer_idx, 0])
        whole = lax.all_gather(moving, "tensor", axis=1, tiled=True)
        outgoing = jnp.where(
            slot_valid[:, None], jnp.take(whole, slot_token, axis=0), jnp.zeros((), jnp.bfloat16)
        )
        slot_inputs = lax.all_to_all(outgoing, "expert", split_axis=0, concat_axis=0, tiled=True)
        activ = expert_activation(slot_inputs, gate_w, up_w)
        partial_value = jnp.dot(activ, down_w, preferred_element_type=jnp.float32)
        reduced = lax.psum_scatter(
            partial_value.astype(jnp.bfloat16), "tensor", scatter_dimension=1, tiled=True
        )
        expert_out = lax.all_to_all(reduced, "expert", split_axis=0, concat_axis=0, tiled=True)
        first_rows = jnp.take(expert_out, first_slot, axis=0).astype(jnp.float32)
        second_rows = jnp.take(expert_out, second_slot, axis=0).astype(jnp.float32)
        stream = (
            stream
            + first_weight[:, None] * first_rows
            + (1.0 - first_weight)[:, None] * second_rows
        )
    return stream.astype(jnp.bfloat16)


def solution(mesh):
    in_specs = (
        P("expert", "tensor"),
        P("expert", None),
        P(None, "tensor"),
        P(None, "tensor", None),
        P(None, "expert", None, "tensor"),
        P(None, "expert", None, "tensor"),
        P(None, "expert", None, "tensor"),
        P(None, "expert", None, "tensor"),
        P(None, "expert", "tensor", None),
        P(None, "expert", "tensor", None),
    )
    out_specs = P("expert", "tensor")
    return jax.shard_map(
        per_device, mesh=mesh, in_specs=in_specs, out_specs=out_specs, check_vma=False
    )
```

profile of v0, /device:TPU:9, one launch (start us, length us, event | category | flops | bytes accessed | tf_op | source)
XLA Modules:
  0.0 558.7 jit_solution(9981842129831694418)
XLA Ops:
  7.6 12.4 %psum.28 = f32[128]{0:T(128)S(1)} all-reduce(f32[128]{0:T(128)S(1)} %fusion.40), channel_id=1, replica_groups=mesh['expert'=16,'tensor'=8] {'tensor'}, use_global_device_ids=true, to_apply=%region_1.2 | all-reduce | flops 128 | bytes 1024 | tf_op jit(solution)/shard_map/psum | solution.py:111
  29.5 7.5 %collective-permute-done.1 = bf16[128,1024]{1,0:T(8,128)(2,1)S(1)} collective-permute-done((bf16[128,1024]{1,0:T(8,128)(2,1)S(1)}, bf16[128,1024]{1,0:T(8,128)(2,1)S(1)}, u32[]{:S(2)}, u32[]{:S(2)}) %collective-permute-start.1) | collective-permute-done | bytes 262176 | tf_op jit(solution)/shard_map/ppermute | solution.py:13
  37.7 8.1 %collective-permute-done.2 = bf16[128,1024]{1,0:T(8,128)(2,1)S(1)} collective-permute-done((bf16[128,1024]{1,0:T(8,128)(2,1)S(1)}, bf16[128,1024]{1,0:T(8,128)(2,1)S(1)}, u32[]{:S(2)}, u32[]{:S(2)}) %collective-permute-start.2) | collective-permute-done | bytes 262176 | tf_op jit(solution)/shard_map/ppermute | solution.py:13
  48.4 25.4 %all-gather.3.cloned.1.call-done = bf16[128,8192]{1,0:T(8,128)(2,1)} async-done(((bf16[128,1024]{1,0:T(8,128)(2,1)}), bf16[128,8192]{1,0:T(8,128)(2,1)}) %all-gather.3.cloned.1.call-update) | async-done | bytes 2097168 | tf_op jit(solution)/shard_map/all_gather | solution.py:125
  73.8 16.7 %gather_fusion = bf16[384,8192]{1,0:T(8,128)(2,1)} fusion(bf16[128,8192]{1,0:T(8,128)(2,1)} %all-gather.3.cloned.1.call-done, s32[1024]{0:T(1024)S(1)} %pad_clamp_fusion.2), kind=kCustom, calls=%fused_computation.clone | custom fusion | bytes 12584448 | tf_op jit(solution)/shard_map/jit(_take)/gather | solution.py:127
  96.7 6.9 %all-to-all-start = ((bf16[16,24,8192]{2,1,0:T(8,128)(2,1)}), bf16[16,24,8192]{2,1,0:T(8,128)(2,1)}, u32[]{:S(2)}, u32[]{:S(2)}) async-start(bf16[16,24,8192]{2,1,0:T(8,128)(2,1)} %bitcast.144), calls=%async_computation | async-start | bytes 12582912 | tf_op jit(solution)/shard_map/all_to_all | solution.py:129
  113.5 6.2 %shift_right_arithmetic.196 = s32[128,8192]{1,0:T(8,128)} reshape(s32[64,2,8192]{2,1,0:T(2,128)} %shift_right_arithmetic.195) | data formatting | bytes 8388608 | tf_op jit(solution)/shard_map/shift_right_arithmetic | solution.py:25
  135.1 58.4 %all-to-all-done = bf16[16,24,8192]{2,1,0:T(8,128)(2,1)} async-done(((bf16[16,24,8192]{2,1,0:T(8,128)(2,1)}), bf16[16,24,8192]{2,1,0:T(8,128)(2,1)}, u32[]{:S(2)}, u32[]{:S(2)}) %all-to-all-start) | async-done | bytes 6291488 | tf_op jit(solution)/shard_map/all_to_all | solution.py:129
  198.8 13.9 %convolution_convert_fusion.1 = bf16[384,8192]{1,0:T(8,128)(2,1)} fusion(s32[128,8192]{1,0:T(8,128)} %shift_right_arithmetic.196, f32[8192]{0:T(1024)S(1)} %bitcast.161, s32[128]{0:T(128)S(1)} %shift_right_arithmetic.187, bf16[384,8192]{1,0:T(8,128)(2,1)} %bitcast.11, bf16[8192,128]{1,0:T(8,128)(2,1)} %bitcast.153, f32[384,128]{1,0:T(8,128)S(1)} %fusion.80), kind=kOutput, calls=%fused_computation.7 | convolution fusion | flops 1620344832 | bytes 19104256 | tf_op jit(solution)/shard_map/dot_general | solution.py:131
  213.7 13.3 %psum.29 = f32[128,16]{0,1:T(8,128)S(1)} all-reduce(f32[128,16]{0,1:T(8,128)S(1)} %fusion.64), channel_id=1, replica_groups=mesh['expert'=16,'tensor'=8] {'tensor'}, use_global_device_ids=true, to_apply=%region_2.3 | all-reduce | flops 2048 | bytes 16384 | tf_op jit(solution)/shard_map/psum | solution.py:115
  227.1 30.1 %reduce-scatter.3.cloned.1.call-done = bf16[384,1024]{1,0:T(8,128)(2,1)} async-done(((bf16[384,8192]{1,0:T(8,128)(2,1)}), bf16[384,1024]{1,0:T(8,128)(2,1)}) %reduce-scatter.3.cloned.1.call-update) | async-done | bytes 786448 | tf_op jit(solution)/shard_map/reduce_scatter | solution.py:132
  257.2 7.2 %all-to-all-start.1 = ((bf16[16,24,1024]{2,1,0:T(8,128)(2,1)}), bf16[16,24,1024]{2,1,0:T(8,128)(2,1)S(1)}, u32[]{:S(2)}, u32[]{:S(2)}) async-start(bf16[16,24,1024]{2,1,0:T(8,128)(2,1)} %bitcast.158), calls=%async_computation.2 | async-start | bytes 1572864 | tf_op jit(solution)/shard_map/all_to_all | solution.py:135
  265.7 10.5 %all-to-all-done.1 = bf16[16,24,1024]{2,1,0:T(8,128)(2,1)S(1)} async-done(((bf16[16,24,1024]{2,1,0:T(8,128)(2,1)}), bf16[16,24,1024]{2,1,0:T(8,128)(2,1)S(1)}, u32[]{:S(2)}, u32[]{:S(2)}) %all-to-all-start.1) | async-done | bytes 786464 | tf_op jit(solution)/shard_map/all_to_all | solution.py:135
  280.8 14.2 %psum.30 = f32[128]{0:T(128)S(1)} all-reduce(f32[128]{0:T(128)S(1)} %get-tuple-element.15), channel_id=1, replica_groups=mesh['expert'=16,'tensor'=8] {'tensor'}, use_global_device_ids=true, to_apply=%region_12.15 | all-reduce | flops 128 | bytes 1024 | tf_op jit(solution)/shard_map/psum | solution.py:111
  304.6 7.5 %collective-permute-done.4 = bf16[128,1024]{1,0:T(8,128)(2,1)S(1)} collective-permute-done((bf16[128,1024]{1,0:T(8,128)(2,1)S(1)}, bf16[128,1024]{1,0:T(8,128)(2,1)S(1)}, u32[]{:S(2)}, u32[]{:S(2)}) %collective-permute-start.4) | collective-permute-done | bytes 262176 | tf_op jit(solution)/shard_map/ppermute | solution.py:13
  312.3 8.1 %collective-permute-done.5 = bf16[128,1024]{1,0:T(8,128)(2,1)S(1)} collective-permute-done((bf16[128,1024]{1,0:T(8,128)(2,1)S(1)}, bf16[128,1024]{1,0:T(8,128)(2,1)S(1)}, u32[]{:S(2)}, u32[]{:S(2)}) %collective-permute-start.5) | collective-permute-done | bytes 262176 | tf_op jit(solution)/shard_map/ppermute | solution.py:13
  321.4 23.8 %all-gather.5.cloned.1.call-done = bf16[128,8192]{1,0:T(8,128)(2,1)} async-done(((bf16[128,1024]{1,0:T(8,128)(2,1)}), bf16[128,8192]{1,0:T(8,128)(2,1)}) %all-gather.5.cloned.1.call-update) | async-done | bytes 2097168 | tf_op jit(solution)/shard_map/all_gather | solution.py:125
  345.2 16.7 %gather_fusion.3 = bf16[384,8192]{1,0:T(8,128)(2,1)} fusion(bf16[128,8192]{1,0:T(8,128)(2,1)} %all-gather.5.cloned.1.call-done, s32[1024]{0:T(1024)S(1)} %pad_clamp_fusion.2), kind=kCustom, calls=%fused_computation.2.clone | custom fusion | bytes 12584448 | tf_op jit(solution)/shard_map/jit(_take)/gather | solution.py:127
  368.1 6.9 %all-to-all-start.2 = ((bf16[16,24,8192]{2,1,0:T(8,128)(2,1)}), bf16[16,24,8192]{2,1,0:T(8,128)(2,1)}, u32[]{:S(2)}, u32[]{:S(2)}) async-start(bf16[16,24,8192]{2,1,0:T(8,128)(2,1)} %bitcast.145), calls=%async_computation.3 | async-start | bytes 12582912 | tf_op jit(solution)/shard_map/all_to_all | solution.py:129
  385.7 79.2 %all-to-all-done.2 = bf16[16,24,8192]{2,1,0:T(8,128)(2,1)} async-done(((bf16[16,24,8192]{2,1,0:T(8,128)(2,1)}), bf16[16,24,8192]{2,1,0:T(8,128)(2,1)}, u32[]{:S(2)}, u32[]{:S(2)}) %all-to-all-start.2) | async-done | bytes 6291488 | tf_op jit(solution)/shard_map/all_to_all | solution.py:129
  469.5 13.9 %convolution_convert_fusion = bf16[384,8192]{1,0:T(8,128)(2,1)} fusion(s32[128,8192]{1,0:T(8,128)} %shift_right_arithmetic.209, f32[8192]{0:T(1024)S(1)} %bitcast.160, s32[128]{0:T(128)S(1)} %shift_right_arithmetic.187, bf16[384,8192]{1,0:T(8,128)(2,1)} %bitcast.30, bf16[8192,128]{1,0:T(8,128)(2,1)} %bitcast.152, f32[384,128]{1,0:T(8,128)S(1)} %fusion.81), kind=kOutput, calls=%fused_computation.6 | convolution fusion | flops 1620344832 | bytes 19104256 | tf_op jit(solution)/shard_map/dot_general | solution.py:131
  483.5 44.5 %reduce-scatter.5.cloned.1.call-done = bf16[384,1024]{1,0:T(8,128)(2,1)} async-done(((bf16[384,8192]{1,0:T(8,128)(2,1)}), bf16[384,1024]{1,0:T(8,128)(2,1)}) %reduce-scatter.5.cloned.1.call-update) | async-done | bytes 786448 | tf_op jit(solution)/shard_map/reduce_scatter | solution.py:132
  528.0 6.9 %all-to-all-start.3 = ((bf16[16,24,1024]{2,1,0:T(8,128)(2,1)}), bf16[16,24,1024]{2,1,0:T(8,128)(2,1)S(1)}, u32[]{:S(2)}, u32[]{:S(2)}) async-start(bf16[16,24,1024]{2,1,0:T(8,128)(2,1)} %bitcast.159), calls=%async_computation.5 | async-start | bytes 1572864 | tf_op jit(solution)/shard_map/all_to_all | solution.py:135
  535.0 14.0 %psum.31 = f32[128,16]{0,1:T(8,128)S(1)} all-reduce(f32[128,16]{0,1:T(8,128)S(1)} %fusion.62), channel_id=1, replica_groups=mesh['expert'=16,'tensor'=8] {'tensor'}, use_global_device_ids=true, to_apply=%region_13.16 | all-reduce | flops 2048 | bytes 16384 | tf_op jit(solution)/shard_map/psum | solution.py:115
  (136 shorter events, 92.3 us)
Async XLA Ops:
  6.5 67.3 %all-gather.3.cloned.1.call-start = ((), (), s32[]{:S(2)}) async-start(), calls=%async_computation.6 | async-start | bytes 2359296 | tf_op jit(solution)/shard_map/all_gather | solution.py:125
  25.2 4.1 collective-permute-start
  29.4 7.6 %collective-permute-start.1 = (bf16[128,1024]{1,0:T(8,128)(2,1)S(1)}, bf16[128,1024]{1,0:T(8,128)(2,1)S(1)}, u32[]{:S(2)}, u32[]{:S(2)}) collective-permute-start(bf16[128,1024]{1,0:T(8,128)(2,1)S(1)} %fusion.61), channel_id=1, source_target_pairs={{0,2},{1,3},{2,0},{3,1},{4,6},{5,7},{6,4},{7,5},{8,10},{9,11},{10,... | collective-permute-start | bytes 786440 | tf_op jit(solution)/shard_map/ppermute | solution.py:13
  37.2 8.6 %collective-permute-start.2 = (bf16[128,1024]{1,0:T(8,128)(2,1)S(1)}, bf16[128,1024]{1,0:T(8,128)(2,1)S(1)}, u32[]{:S(2)}, u32[]{:S(2)}) collective-permute-start(bf16[128,1024]{1,0:T(8,128)(2,1)S(1)} %fusion.47), channel_id=1, source_target_pairs={{0,4},{1,5},{2,6},{3,7},{4,0},{5,1},{6,2},{7,3},{8,12},{9,13},{10,... | collective-permute-start | bytes 786440 | tf_op jit(solution)/shard_map/ppermute | solution.py:13
  48.4 42.1 %copy-start.11 = (pred[384]{0:T(512)(128)(4,1)}, pred[384]{0:T(512)(128)(4,1)S(1)}, u32[]{:S(2)}) copy-start(pred[384]{0:T(512)(128)(4,1)S(1)} %get-tuple-element.39) | copy-start | bytes 1156
  48.4 42.1 %copy-start.13 = (pred[384]{0:T(512)(128)(4,1)}, pred[384]{0:T(512)(128)(4,1)S(1)}, u32[]{:S(2)}) copy-start(pred[384]{0:T(512)(128)(4,1)S(1)} %get-tuple-element.40) | copy-start | bytes 1156
  96.7 96.9 %all-to-all-start = ((bf16[16,24,8192]{2,1,0:T(8,128)(2,1)}), bf16[16,24,8192]{2,1,0:T(8,128)(2,1)}, u32[]{:S(2)}, u32[]{:S(2)}) async-start(bf16[16,24,8192]{2,1,0:T(8,128)(2,1)} %bitcast.144), calls=%async_computation | async-start | bytes 12582912 | tf_op jit(solution)/shard_map/all_to_all | solution.py:129
  103.5 153.7 %reduce-scatter.3.cloned.1.call-start = ((), (), s32[]{:S(2)}) async-start(), calls=%async_computation.7 | async-start | bytes 7077888 | tf_op jit(solution)/shard_map/reduce_scatter | solution.py:132
  257.2 38.8 %copy-start.9 = (bf16[32,32,1]{0,1,2:T(8,128)(2,1)S(1)}, bf16[32,32,1]{0,1,2:T(8,128)(2,1)}, u32[]{:S(2)}) copy-start(bf16[32,32,1]{0,1,2:T(8,128)(2,1)} %constant.101) | copy-start | bytes 6148
  257.2 19.0 %all-to-all-start.1 = ((bf16[16,24,1024]{2,1,0:T(8,128)(2,1)}), bf16[16,24,1024]{2,1,0:T(8,128)(2,1)S(1)}, u32[]{:S(2)}, u32[]{:S(2)}) async-start(bf16[16,24,1024]{2,1,0:T(8,128)(2,1)} %bitcast.158), calls=%async_computation.2 | async-start | bytes 1572864 | tf_op jit(solution)/shard_map/all_to_all | solution.py:135
  264.4 80.8 %all-gather.5.cloned.1.call-start = ((), (), s32[]{:S(2)}) async-start(), calls=%async_computation.8 | async-start | bytes 2359296 | tf_op jit(solution)/shard_map/all_gather | solution.py:125
  300.5 3.9 collective-permute-start.3
  304.5 7.6 %collective-permute-start.4 = (bf16[128,1024]{1,0:T(8,128)(2,1)S(1)}, bf16[128,1024]{1,0:T(8,128)(2,1)S(1)}, u32[]{:S(2)}, u32[]{:S(2)}) collective-permute-start(bf16[128,1024]{1,0:T(8,128)(2,1)S(1)} %fusion.60), channel_id=1, source_target_pairs={{0,2},{1,3},{2,0},{3,1},{4,6},{5,7},{6,4},{7,5},{8,10},{9,11},{10,... | collective-permute-start | bytes 786440 | tf_op jit(solution)/shard_map/ppermute | solution.py:13
  312.2 8.2 %collective-permute-start.5 = (bf16[128,1024]{1,0:T(8,128)(2,1)S(1)}, bf16[128,1024]{1,0:T(8,128)(2,1)S(1)}, u32[]{:S(2)}, u32[]{:S(2)}) collective-permute-start(bf16[128,1024]{1,0:T(8,128)(2,1)S(1)} %fusion.46), channel_id=1, source_target_pairs={{0,4},{1,5},{2,6},{3,7},{4,0},{5,1},{6,2},{7,3},{8,12},{9,13},{10,... | collective-permute-start | bytes 786440 | tf_op jit(solution)/shard_map/ppermute | solution.py:13
  321.4 40.5 %copy-start.12 = (pred[384]{0:T(512)(128)(4,1)S(1)}, pred[384]{0:T(512)(128)(4,1)}, u32[]{:S(2)}) copy-start(pred[384]{0:T(512)(128)(4,1)} %copy-done.11) | copy-start | bytes 1156
  321.4 40.5 %copy-start.14 = (pred[384]{0:T(512)(128)(4,1)S(1)}, pred[384]{0:T(512)(128)(4,1)}, u32[]{:S(2)}) copy-start(pred[384]{0:T(512)(128)(4,1)} %copy-done.13) | copy-start | bytes 1156
  368.1 96.9 %all-to-all-start.2 = ((bf16[16,24,8192]{2,1,0:T(8,128)(2,1)}), bf16[16,24,8192]{2,1,0:T(8,128)(2,1)}, u32[]{:S(2)}, u32[]{:S(2)}) async-start(bf16[16,24,8192]{2,1,0:T(8,128)(2,1)} %bitcast.145), calls=%async_computation.3 | async-start | bytes 12582912 | tf_op jit(solution)/shard_map/all_to_all | solution.py:129
  374.9 153.0 %reduce-scatter.5.cloned.1.call-start = ((), (), s32[]{:S(2)}) async-start(), calls=%async_computation.9 | async-start | bytes 7077888 | tf_op jit(solution)/shard_map/reduce_scatter | solution.py:132
  379.5 85.4 %copy-start = (bf16[64,128,128]{2,1,0:T(8,128)(2,1)S(1)}, bf16[64,128,128]{2,1,0:T(8,128)(2,1)}, u32[]{:S(2)}) copy-start(bf16[64,128,128]{2,1,0:T(8,128)(2,1)} %get-tuple-element.35) | copy-start | bytes 6291460
  483.4 51.4 %copy-start.3 = (bf16[128,1024]{1,0:T(8,128)(2,1)S(1)}, bf16[128,1024]{1,0:T(8,128)(2,1)}, u32[]{:S(2)}) copy-start(bf16[128,1024]{1,0:T(8,128)(2,1)} %copy-done.2) | copy-start | bytes 786436
  483.4 65.6 %copy-start.16 = (s32[128]{0:T(128)S(1)}, s32[128]{0:T(128)}, u32[]{:S(2)}) copy-start(s32[128]{0:T(128)} %copy-done.15) | copy-start | bytes 1540
  483.5 65.6 %copy-start.18 = (s32[128]{0:T(128)S(1)}, s32[128]{0:T(128)}, u32[]{:S(2)}) copy-start(s32[128]{0:T(128)} %copy-done.17) | copy-start | bytes 1540
  483.5 67.3 %copy-start.10 = (pred[128]{0:T(512)(128)(4,1)S(1)}, pred[128]{0:T(512)(128)(4,1)}, u32[]{:S(2)}) copy-start(pred[128]{0:T(512)(128)(4,1)} %get-tuple-element.44) | copy-start | bytes 388
  528.0 21.1 %all-to-all-start.3 = ((bf16[16,24,1024]{2,1,0:T(8,128)(2,1)}), bf16[16,24,1024]{2,1,0:T(8,128)(2,1)S(1)}, u32[]{:S(2)}, u32[]{:S(2)}) async-start(bf16[16,24,1024]{2,1,0:T(8,128)(2,1)} %bitcast.159), calls=%async_computation.5 | async-start | bytes 1572864 | tf_op jit(solution)/shard_map/all_to_all | solution.py:135
  (10 other events, 112.3 us)
Sparse Core Ops, SparseCore 0:
  46.9 26.8 all-gather.2
  212.8 44.3 reduce-scatter.2
  321.5 23.6 all-gather.4
  483.6 44.3 reduce-scatter.4
where the time goes:
time: 564 us; the launch traced here: 559 us
  waiting for transfers between devices  305 us (54%)
  local copies, waits for them, and re-layouts  80.7 us (14%)
  blocking collectives  54 us (10%)
  matrix products  42.5 us (8%)
  starting transfers between devices  34.7 us (6%)
  other arithmetic  27.3 us (5%)
  between operations  14 us (2%)
    all_to_all x2, waiting for transfers between devices, per_device(): lax.all_to_all(outgoing, 'expert', split_axis=0, concat_axis=0, tiled=True)  138 us
    reduce_scatter x2, waiting for transfers between devices, per_device(): lax.psum_scatter(partial_value.astype(jnp.bfloat16), 'tensor', scatter_di...  74.6 us
    all_gather x2, waiting for transfers between devices, per_device(): whole = lax.all_gather(moving, 'tensor', axis=1, tiled=True)  49.2 us
    shift_right_arithmetic x13, local copies, waits for them, and re-layouts, unpack(): jnp.right_shift(words[:, None, :], shifts[None, :, None])  35.5 us
    ppermute x6, waiting for transfers between devices, from_partner(): lax.ppermute(shard, axis, [(i, i ^ 1 << stride) for i in range(lax.axis_s...  33.5 us
    gather x2, local copies, waits for them, and re-layouts, per_device(): jnp.take(whole, slot_token, axis=0)  33.4 us
    dot_general x2, matrix products, per_device(): partial_value = jnp.dot(activ, down_w, preferred_element_type=jnp.float32)  27.9 us
    psum x2, blocking collectives, per_device(): lax.psum(jnp.dot(normed, router_weight[layer_idx], preferred_element_type...  27.3 us
  transfers between devices with their start and end apart: 14, of which 13 were waited for; matrix products, arithmetic and copies ran while one was open for 8% of the time, Pallas kernels for 0%

commit v1 on v0

v1 whole, which is shorter than its diff:
```python
import functools
import math

import jax
import jax.numpy as jnp
from jax import lax
from jax.experimental import pallas as pl
from jax.experimental.pallas import tpu as pltpu
from jax.sharding import PartitionSpec as P

LAYERS = 2
TOK = 128
WIDTH = 1024
HALF = 512
CAP = 24
CHUNK = 2 * CAP
ROWS = 16 * CHUNK
GROUP = 4 * CHUNK
VIA_UP = (0, 3)
VIA_DOWN = (1, 2)
MESH = pl.DeviceIdType.MESH
F32 = jnp.float32
BF16 = jnp.bfloat16
I32 = jnp.int32


def dot(a, b):
    return jnp.dot(a, b, preferred_element_type=F32)


def back(a, b):
    return ((-a) % 4) * 4 + (-b) % 4


def iota(shape, dim):
    return lax.broadcasted_iota(I32, shape, dim)


def walsh(values):
    values = list(values)
    for bit in (1, 2, 4):
        for i in range(8):
            if not i & bit:
                low, high = values[i], values[i | bit]
                values[i], values[i | bit] = low + high, low - high
    return values


def rows_of(group):
    return pl.ds(group * GROUP, GROUP)


def kernel(
    tok_ref, routes_ref, gain_ref, rw_ref, gc_hbm, gs_ref, uc_hbm, us_ref, dc_hbm, ds_ref,
    out_ref,
    stream, had, cg, cu, cd, wp, wd, gath, pick, xr, sl, xf, acc, actx, actp,
    own, pk1, sibr, rh, rf, ret, ex, fw_ref,
    code_sem, ex_s, ex_r, disp_s, disp_r, ag_s, ag_r, rs_s, rs_r, ret_s, ret_r,
):
    e = lax.axis_index("expert")
    t = lax.axis_index("tensor")
    z, y = e // 4, e % 4
    x, c = t // 2, t % 2

    def expert_at(a, b):
        return {"expert": ((z + a) % 4) * 4 + (y + b) % 4, "tensor": t}

    def tensor_at(index):
        return {"expert": e, "tensor": index}

    sibling = tensor_at(2 * x + (1 - c))
    up = tensor_at(2 * ((x + 1) % 4) + c)
    down = tensor_at(2 * ((x + 3) % 4) + c)

    def block(d, k):
        core = c if k == 0 else 1 - c
        return 2 * ((x + d) % 4) + core

    def remote(src, dst, ssem, rsem, device):
        return pltpu.make_async_remote_copy(
            src_ref=src, dst_ref=dst, send_sem=ssem, recv_sem=rsem,
            device_id=device, device_id_type=MESH,
        )

    def code_copies(l):
        return [
            pltpu.make_async_copy(gc_hbm.at[l], cg, code_sem.at[0]),
            pltpu.make_async_copy(uc_hbm.at[l], cu, code_sem.at[1]),
            pltpu.make_async_copy(dc_hbm.at[l], cd, code_sem.at[2]),
        ]

    barrier = pltpu.get_barrier_semaphore()
    for a in range(4):
        for b in range(4):
            if a or b:
                pl.semaphore_signal(
                    barrier, inc=1, device_id=expert_at(a, b), device_id_type=MESH
                )
    for k in range(1, 8):
        pl.semaphore_signal(
            barrier, inc=1, device_id=tensor_at((t + k) % 8), device_id_type=MESH
        )

    eye = (iota((TOK, TOK), 0) == iota((TOK, TOK), 1)).astype(F32)
    below = (iota((TOK, TOK), 0) > iota((TOK, TOK), 1)).astype(BF16)
    lanes = iota((TOK, 16), 1)
    picks, rels = [], []
    for k in range(2):
        named = routes_ref[:, k : k + 1]
        picks.append((named == lanes).astype(F32))
        rels.append((((named // 4) - z + 4) % 4) * 4 + ((named % 4) - y + 4) % 4)
    earlier = dot(below, (picks[0] + picks[1]).astype(BF16))
    slots = []
    for k in range(2):
        rank = jnp.sum(picks[k] * earlier, axis=1, keepdims=True)
        slots.append(rels[k].astype(F32) * CAP + rank)
    slot_rows = [jnp.sum(eye * s, axis=0, keepdims=True).astype(I32) for s in slots]
    slot_cols = [s.astype(I32) for s in slots]
    sign = picks[0] - picks[1]

    row = iota((ROWS, 1), 0)
    chunk = row // CHUNK
    inner = row - chunk * CHUNK
    row_half = (inner >= CAP).astype(I32)
    row_slot = chunk * CAP + inner - row_half * CAP
    col_half = (iota((1, 2 * TOK), 1) >= TOK).astype(I32)
    both = [jnp.concatenate([s, s], axis=1) for s in slot_rows]
    hit = (row_half == col_half) & ((row_slot == both[0]) | (row_slot == both[1]))
    gath[...] = hit.astype(F32).astype(BF16)

    lane = iota((1, ROWS), 1)
    lane_chunk = lane // CHUNK
    lane_inner = lane - lane_chunk * CHUNK
    lane_half = (lane_inner >= CAP).astype(I32)
    lane_slot = lane_chunk * CAP + lane_inner - lane_half * CAP
    for k in range(2):
        for h in range(2):
            hit = (lane_half == h) & (lane_slot == slot_cols[k])
            pick[k, pl.ds(h * TOK, TOK), :] = hit.astype(F32).astype(BF16)

    @pl.loop(0, 32)
    def _(i):
        at = pl.multiple_of(i * 32, 32)
        r = iota((32, WIDTH), 0) + at
        j = iota((32, WIDTH), 1)
        v = r & (2 * (j & (HALF - 1)) + (j >> 9))
        v = v ^ (v >> 8)
        v = v ^ (v >> 4)
        v = v ^ (v >> 2)
        v = v ^ (v >> 1)
        had[pl.ds(at, 32), :] = (1 - 2 * (v & 1)).astype(F32).astype(BF16)

    stream[...] = tok_ref[...].astype(F32)
    for copy in code_copies(0):
        copy.start()
    pl.semaphore_wait(barrier, 22)

    def exchange(l, which, column):
        ex[l, which, 0] = jnp.broadcast_to(
            jnp.sum(eye * column, axis=0, keepdims=True), (8, TOK)
        )
        copies = [
            remote(
                ex.at[l, which, 0], ex.at[l, which, k], ex_s.at[l, which, k],
                ex_r.at[l, which, k], tensor_at((t + k) % 8),
            )
            for k in range(1, 8)
        ]
        for copy in copies:
            copy.start()
        return copies

    def exchanged(l, which, copies):
        for copy in copies:
            copy.wait_recv()
        total = ex[l, which, 0]
        for k in range(1, 8):
            total = total + ex[l, which, k]
        return jnp.sum(eye * total[0:1, :], axis=1, keepdims=True)

    def prepare_in(l, step):
        at = pl.multiple_of(step * 32, 32)
        for kind, (codes, scales) in enumerate(((cg, gs_ref), (cu, us_ref))):
            words = [codes[pl.ds(m * HALF + at, 32), :] for m in range(8)]
            shifts = [10 - scales[l, pl.ds(m * 8 + step // 2, 1), :] for m in range(8)]
            for k in range(2):
                values = walsh(
                    ((((w >> (4 * k)) & 15) - 8) << s) for w, s in zip(words, shifts)
                )
                column = k * 256 + kind * 128
                for n in range(8):
                    wp[n, pl.ds(at, 32), column : column + 128] = (
                        values[n].astype(F32).astype(BF16)
                    )

    def prepare_out(l, n):
        for h in range(2):
            at = pl.multiple_of(n * WIDTH + h * HALF, HALF)
            words = cd[:, pl.ds(at, HALF)]
            shift = 8 - ds_ref[pl.ds(l, 1), pl.ds(at, HALF)]
            for k in range(2):
                value = (((words >> (4 * k)) & 15) - 8) << shift
                wd[n, pl.ds(h * 128 + k * 64, 64), :] = (
                    value.astype(F32) * (2.0**-8)
                ).astype(BF16)

    def multiply_in(l, d, k, first=False):
        n = block(d, k)

        @pl.loop(0, 4)
        def _(g):
            at = pl.ds(pl.multiple_of(g * GROUP, GROUP), GROUP)
            value = dot(xf[l, d, k, at, :], wp[n])
            if first:
                acc[at, :] = value
            else:
                acc[at, :] += value

    def multiply_out(d, k):
        n = block(d, k)
        target = own if k == 0 else pk1

        @pl.loop(0, 4)
        def _(g):
            at = pl.ds(pl.multiple_of(g * GROUP, GROUP), GROUP)
            target[d, at, :] = dot(actp[at, :], wd[n]).astype(BF16)

    def add_into(d, g, parts):
        total = own[d, rows_of(g), :].astype(F32)
        for part in parts:
            total = total + part.astype(F32)
        own[d, rows_of(g), :] = total.astype(BF16)

    mix = (
        (iota((256, 256), 0) >> 7 == iota((256, 256), 1) >> 7)
        & (
            iota((256, 256), 1) & 127
            == ((iota((256, 256), 0) & 127) >> 1) + 64 * (iota((256, 256), 0) & 1)
        )
    ).astype(F32).astype(BF16)

    def layer(l, carry):
        sends = []
        st = stream[...]
        squares = exchange(l, 0, jnp.sum(st * st, axis=1, keepdims=True))
        sends += squares
        square = exchanged(l, 0, squares)
        normed = (
            st * lax.rsqrt(square / (8 * WIDTH) + 1e-05) * gain_ref[pl.ds(l, 1), :]
        ).astype(BF16)
        for h in range(2):
            xr[pl.ds(h * TOK, TOK), :] = dot(
                normed, had[:, h * HALF : (h + 1) * HALF]
            ).astype(BF16)

        dispatch = {}
        for a in (0, 1, 3, 2):
            value = dot(gath[rows_of(a), :], xr[...]).astype(BF16)
            sl[rows_of(a), :] = value
            if a == 0:
                xf[l, 0, 0, 0:CHUNK, :] = value[0:CHUNK, :]
            for b in range(4):
                if a or b:
                    j = back(a, b)
                    dispatch[j] = remote(
                        sl.at[pl.ds((a * 4 + b) * CHUNK, CHUNK), :],
                        xf.at[l, 0, 0, pl.ds(j * CHUNK, CHUNK), :],
                        disp_s.at[l, j], disp_r.at[l, j], expert_at(a, b),
                    )
                    dispatch[j].start()
        sends += list(dispatch.values())

        logits = dot(normed, rw_ref[l])
        shares = exchange(l, 1, jnp.sum(logits * sign, axis=1, keepdims=True))
        sends += shares

        codes = code_copies(l)
        codes[0].wait()
        codes[1].wait()

        def gather(kind, g, src, dst, device):
            return remote(
                xf.at[(l,) + src + (rows_of(g),)], xf.at[(l,) + dst + (rows_of(g),)],
                ag_s.at[l, kind, g], ag_r.at[l, kind, g], device,
            )

        to_sib, to_up, to_down = {}, {}, {}
        for i, g in enumerate((0, 3, 1, 2)):
            @pl.loop(4 * i, 4 * i + 4)
            def _(step):
                prepare_in(l, step)

            for b in range(4):
                if g or b:
                    dispatch[g * 4 + b].wait_recv()
            to_up[g] = gather(1, g, (0, 0), (3, 0), up)
            to_down[g] = gather(2, g, (0, 0), (1, 0), down)
            to_sib[g] = gather(0, g, (0, 0), (0, 1), sibling)
            to_up[g].start()
            to_down[g].start()
            to_sib[g].start()
        codes[2].wait()

        multiply_in(l, 0, 0, first=True)

        @pl.loop(0, 8)
        def _(n):
            prepare_out(l, n)

        @pl.when(l + 1 < LAYERS)
        def _():
            for copy in code_copies(l + 1):
                copy.start()

        below_sib, above_sib, two = {}, {}, {}
        for g in (0, 3, 1, 2):
            to_up[g].wait_recv()
            if g in VIA_UP:
                two[g] = gather(5, g, (3, 0), (2, 0), up)
                two[g].start()
            below_sib[g] = gather(3, g, (3, 0), (3, 1), sibling)
            below_sib[g].start()
            to_down[g].wait_recv()
            if g in VIA_DOWN:
                two[g] = gather(5, g, (1, 0), (2, 0), down)
                two[g].start()
            above_sib[g] = gather(4, g, (1, 0), (1, 1), sibling)
            above_sib[g].start()
        multiply_in(l, 3, 0)
        multiply_in(l, 1, 0)
        for g in range(4):
            to_sib[g].wait_recv()
        multiply_in(l, 0, 1)
        two_sib = {}
        for g in (0, 3, 1, 2):
            two[g].wait_recv()
            two_sib[g] = gather(6, g, (2, 0), (2, 1), sibling)
            two_sib[g].start()
        for g in range(4):
            below_sib[g].wait_recv()
        multiply_in(l, 3, 1)
        for g in range(4):
            above_sib[g].wait_recv()
        multiply_in(l, 1, 1)
        multiply_in(l, 2, 0)
        for g in range(4):
            two_sib[g].wait_recv()
        multiply_in(l, 2, 1)
        for table in (to_sib, to_up, to_down, below_sib, above_sib, two, two_sib):
            sends += list(table.values())

        factor = 2.0**-10 / math.sqrt(8 * WIDTH)
        zero = jnp.zeros((CAP, 128), F32)

        @pl.loop(0, 16)
        def _(j):
            even = pl.ds(pl.multiple_of(j * CHUNK, 8), CAP)
            odd = pl.ds(pl.multiple_of(j * CHUNK + CAP, 8), CAP)
            total = (acc[even, 0:256] + acc[odd, 256:512]) * factor
            gate, value = total[:, 0:128], total[:, 128:256]
            act = gate / (1.0 + jnp.exp(-gate)) * value
            actx[even, 0:128] = act
            actx[even, 128:256] = zero
            actx[odd, 0:128] = zero
            actx[odd, 128:256] = act

        actp[...] = dot(actx[...].astype(BF16), mix).astype(BF16)

        def scatter(kind, g, src, dst, device):
            return remote(src, dst, rs_s.at[l, kind, g], rs_r.at[l, kind, g], device)

        sib = {}

        def to_sibling(d):
            multiply_out(d, 1)
            sib[d] = scatter(0, d, pk1.at[d], sibr.at[l, d], sibling)
            sib[d].start()

        to_sibling(2)
        multiply_out(2, 0)
        to_sibling(1)
        sib[2].wait_recv()
        half, whole_up, whole_down = {}, {}, {}
        for g in (3, 2, 0, 1):
            add_into(2, g, [sibr[l, 2, rows_of(g), :]])
            half[g] = scatter(
                1, g, own.at[2, rows_of(g), :], rh.at[l, rows_of(g), :],
                up if g in VIA_UP else down,
            )
            half[g].start()
        multiply_out(1, 0)
        to_sibling(3)
        multiply_out(3, 0)

        def send_whole(d, g, parts):
            add_into(d, g, [sibr[l, d, rows_of(g), :]] + parts)
            table, kind, device = (
                (whole_up, 2, up) if d == 1 else (whole_down, 3, down)
            )
            table[g] = scatter(
                kind, g, own.at[d, rows_of(g), :], rf.at[l, kind - 2, rows_of(g), :], device
            )
            table[g].start()

        sib[1].wait_recv()
        send_whole(1, 2, [])
        send_whole(1, 1, [])
        sib[3].wait_recv()
        send_whole(3, 3, [])
        send_whole(3, 0, [])
        to_sibling(0)
        multiply_out(0, 0)
        for g in (3, 2, 0, 1):
            half[g].wait_recv()
            send_whole(1 if g in VIA_UP else 3, g, [rh[l, rows_of(g), :]])
        sib[0].wait_recv()
        returns = {}
        for g in (3, 2, 0, 1):
            whole_up[g].wait_recv()
            whole_down[g].wait_recv()
            add_into(
                0, g,
                [sibr[l, 0, rows_of(g), :], rf[l, 0, rows_of(g), :], rf[l, 1, rows_of(g), :]],
            )
            for b in range(4):
                if g or b:
                    j = back(g, b)
                    returns[j] = remote(
                        own.at[0, pl.ds((g * 4 + b) * CHUNK, CHUNK), :],
                        ret.at[l, pl.ds(j * CHUNK, CHUNK), :],
                        ret_s.at[l, j], ret_r.at[l, j], expert_at(g, b),
                    )
                    returns[j].start()
                else:
                    ret[l, 0:CHUNK, :] = own[0, 0:CHUNK, :]
        for table in (sib, half, whole_up, whole_down, returns):
            sends += list(table.values())

        diff = exchanged(l, 1, shares)
        weight = 1.0 / (1.0 + jnp.exp(-diff))
        for j in range(1, 16):
            returns[j].wait_recv()
        for h in range(2):
            part = pl.ds(h * TOK, TOK)
            first = dot(pick[0, part, :], ret[l])
            second = dot(pick[1, part, :], ret[l])
            columns = slice(h * HALF, (h + 1) * HALF)
            stream[:, columns] = (
                stream[:, columns] + weight * first + (1.0 - weight) * second
            )
        for copy in sends:
            copy.wait_send()
        return carry

    lax.fori_loop(0, LAYERS, layer, 0)
    out_ref[...] = stream[...].astype(BF16)


def per_device(
    tokens, routes, norm_gain, router_weight, gate_codes, gate_scales, up_codes, up_scales,
    down_codes, down_scales,
):
    vmem = pl.BlockSpec(memory_space=pltpu.VMEM)
    anywhere = pl.BlockSpec(memory_space=pl.ANY)
    dma = pltpu.SemaphoreType.DMA
    return pl.pallas_call(
        kernel,
        out_shape=jax.ShapeDtypeStruct((TOK, WIDTH), BF16),
        in_specs=[
            vmem, vmem, vmem, vmem, anywhere, vmem, anywhere, vmem, anywhere, vmem,
        ],
        out_specs=vmem,
        scratch_shapes=[
            pltpu.VMEM((TOK, WIDTH), F32),
            pltpu.VMEM((WIDTH, WIDTH), BF16),
            pltpu.VMEM((4096, 128), I32),
            pltpu.VMEM((4096, 128), I32),
            pltpu.VMEM((64, 8192), I32),
            pltpu.VMEM((8, HALF, HALF), BF16),
            pltpu.VMEM((8, 256, HALF), BF16),
            pltpu.VMEM((ROWS, 2 * TOK), BF16),
            pltpu.VMEM((2, 2 * TOK, ROWS), BF16),
            pltpu.VMEM((2 * TOK, HALF), BF16),
            pltpu.VMEM((ROWS, HALF), BF16),
            pltpu.VMEM((LAYERS, 4, 2, ROWS, HALF), BF16),
            pltpu.VMEM((ROWS, HALF), F32),
            pltpu.VMEM((ROWS, 256), F32),
            pltpu.VMEM((ROWS, 256), BF16),
            pltpu.VMEM((4, ROWS, HALF), BF16),
            pltpu.VMEM((4, ROWS, HALF), BF16),
            pltpu.VMEM((LAYERS, 4, ROWS, HALF), BF16),
            pltpu.VMEM((LAYERS, ROWS, HALF), BF16),
            pltpu.VMEM((LAYERS, 2, ROWS, HALF), BF16),
            pltpu.VMEM((LAYERS, ROWS, HALF), BF16),
            pltpu.VMEM((LAYERS, 2, 8, 8, TOK), F32),
            pltpu.VMEM((TOK, 128), F32),
            dma((3,)),
            dma((LAYERS, 2, 8)), dma((LAYERS, 2, 8)),
            dma((LAYERS, 16)), dma((LAYERS, 16)),
            dma((LAYERS, 7, 4)), dma((LAYERS, 7, 4)),
            dma((LAYERS, 4, 4)), dma((LAYERS, 4, 4)),
            dma((LAYERS, 16)), dma((LAYERS, 16)),
        ],
        compiler_params=pltpu.CompilerParams(
            collective_id=0, has_side_effects=True, vmem_limit_bytes=60 << 20
        ),
        name="moe_layers",
    )(
        tokens, routes, norm_gain, router_weight, gate_codes.reshape(LAYERS, 4096, 128),
        gate_scales.reshape(LAYERS, 64, 128), up_codes.reshape(LAYERS, 4096, 128),
        up_scales.reshape(LAYERS, 64, 128), down_codes.reshape(LAYERS, 64, 8192),
        down_scales.reshape(LAYERS, 8192),
    )


def solution(mesh):
    in_specs = (
        P("expert", "tensor"),
        P("expert", None),
        P(None, "tensor"),
        P(None, "tensor", None),
        P(None, "expert", None, "tensor"),
        P(None, "expert", None, "tensor"),
        P(None, "expert", None, "tensor"),
        P(None, "expert", None, "tensor"),
        P(None, "expert", "tensor", None),
        P(None, "expert", "tensor", None),
    )
    return jax.shard_map(
        per_device, mesh=mesh, in_specs=in_specs, out_specs=P("expert", "tensor"),
        check_vma=False,
    )
```

time: 564 us -> 183 us (0.32)
  waiting for transfers between devices: 305 us -> 0 us
  Pallas kernels: 0 us -> 174 us
  local copies, waits for them, and re-layouts: 80.7 us -> 6.43 us
  blocking collectives: 54 us -> 0 us
  matrix products: 42.5 us -> 0 us
  starting transfers between devices: 34.7 us -> 0 us
  other arithmetic: 27.3 us -> 0 us
  between operations: 14 us -> 0.01 us
    pallas_call x0 -> x1, Pallas kernels: none -> 174 us  [per_device(): pl.pallas_call(kernel, out_shape=jax.ShapeDtypeStruct((TOK, WIDTH), BF16)...]
    all_to_all x4 -> x0, waiting for transfers between devices: 148 us -> none  [the longest x2 138 us: per_device(): lax.all_to_all(outgoing, 'expert', split_axis=0, concat_axis=0, tiled=True)]
    reduce_scatter x2 -> x0, waiting for transfers between devices: 74.6 us -> none  [per_device(): lax.psum_scatter(partial_value.astype(jnp.bfloat16), 'tensor', scatter_di...]
    psum x4 -> x0, blocking collectives: 54 us -> none  [the longest x2 27.3 us: per_device(): lax.psum(jnp.dot(normed, router_weight[layer_idx], preferred_element_type...]
    all_gather x2 -> x0, waiting for transfers between devices: 49.2 us -> none  [per_device(): whole = lax.all_gather(moving, 'tensor', axis=1, tiled=True)]
    dot_general x10 -> x0, matrix products: 42.5 us -> none  [the longest x2 27.9 us: per_device(): partial_value = jnp.dot(activ, down_w, preferred_element_type=jnp.float32)]
    gather x6 -> x0, local copies, waits for them, and re-layouts: 38.2 us -> none  [the longest x2 33.4 us: per_device(): jnp.take(whole, slot_token, axis=0)]
    shift_right_arithmetic x13 -> x0, local copies, waits for them, and re-layouts: 35.5 us -> none  [unpack(): jnp.right_shift(words[:, None, :], shifts[None, :, None])]
  transfers between devices with their start and end apart: 14 -> 0, of which waited for: 13 -> 0; matrix products, arithmetic and copies ran while one was open for 8% -> 0% of each run, Pallas kernels for 0% -> 0%
where the time goes in v1:
time: 183 us; the launch traced here: 180 us
  Pallas kernels  174 us (95%)
  local copies, waits for them, and re-layouts  6.43 us (4%)
    pallas_call x1, Pallas kernels, per_device(): pl.pallas_call(kernel, out_shape=jax.ShapeDtypeStruct((TOK, WIDTH), BF16)...  174 us
    unnamed x4, local copies, waits for them, and re-layouts  6.43 us

profile of v1, /device:TPU:9, one launch (start us, length us, event | category | flops | bytes accessed | tf_op | source)
XLA Modules:
  0.0 180.4 jit_solution(4912632533121728634)
XLA Ops:
  0.0 1.4 copy.11.routes_ref
  1.4 1.5 copy.15
  2.9 1.8 %copy.12.rw_ref = bf16[2,1024,16]{2,1,0:T(8,128)(2,1)} copy(bf16[2,1024,16]{1,2,0:T(8,128)(2,1)} %param.13) | data formatting | bytes 131072 | tf_op args[3]
  4.8 174.0 %moe_layers.1 = bf16[128,1024]{1,0:T(8,128)(2,1)} custom-call(bf16[128,1024]{1,0:T(8,128)(2,1)} %tok_ref.1, s32[128,2]{1,0:T(8,128)} %copy.11.routes_ref, f32[2,1024]{1,0:T(2,128)} %gain_ref.1, bf16[2,1024,16]{2,1,0:T(8,128)(2,1)} %copy.12.rw_ref, s32[2,4096,128]{2,1,0:T(8,128)} %bitcast.8, s32[2,64,128]{2,1,0:T(8,128)} %bitcast.12, ...), custom_call_target="tpu_custom_call" | custom-call | tf_op jit(solution)/shard_map/moe_layers/pallas_call | solution.py:466
  178.7 1.7 copy.17

commit v2 on v1

v2 whole, which is shorter than its diff:
```python
import functools
import math

import jax
import jax.numpy as jnp
from jax import lax
from jax.experimental import pallas as pl
from jax.experimental.pallas import tpu as pltpu
from jax.sharding import PartitionSpec as P

LAYERS = 2
TOK = 128
WIDTH = 1024
HALF = 512
CAP = 24
CHUNK = 2 * CAP
ROWS = 16 * CHUNK
GROUP = 4 * CHUNK
PART = 2 * GROUP
MESH = pl.DeviceIdType.MESH
F32 = jnp.float32
BF16 = jnp.bfloat16
I32 = jnp.int32


def dot(a, b):
    return jnp.dot(a, b, preferred_element_type=F32)


def place(z, y):
    return lax.rem(z + y, 2) * 8 + z * 2 + lax.div(y, 2)


def chunk_at(index):
    return pl.ds(pl.multiple_of(index * CHUNK, CHUNK), CHUNK)


def iota(shape, dim):
    return lax.broadcasted_iota(I32, shape, dim)


def walsh(values):
    values = list(values)
    for bit in (1, 2, 4):
        for i in range(8):
            if not i & bit:
                low, high = values[i], values[i | bit]
                values[i], values[i | bit] = low + high, low - high
    return values


def rows_of(group, count=1):
    return pl.ds(group * GROUP, count * GROUP)


def kernel(
    tok_ref, routes_ref, gain_ref, rw_ref, gc_hbm, gs_ref, uc_hbm, us_ref, dc_hbm, ds_ref,
    out_ref,
    stream, had, cg, cu, cd, wp, wd, gath, pick, xr, sl, xf, acc, actx, actp,
    own, pk1, sibr, rh, rf, ret, ex, weights, scale_out, scales,
    code_sem, ex_s, ex_r, scale_s, scale_r, disp_s, disp_r, ag_s, ag_r, rs_s, rs_r, ret_s, ret_r,
):
    e = lax.axis_index("expert")
    t = lax.axis_index("tensor")
    z, y = lax.div(e, 4), lax.rem(e, 4)
    x, c = lax.div(t, 2), lax.rem(t, 2)
    zs = [z] + [lax.rem(z + a, 4) for a in range(1, 4)]
    ys = [y] + [lax.rem(y + b, 4) for b in range(1, 4)]
    parity = lax.rem(z + y, 2)
    mine = place(z, y)
    xs = [x * 2] + [lax.rem(x + d, 4) * 2 for d in range(1, 4)]
    cores = [c, 1 - c]

    def expert_at(a, b):
        return {"expert": zs[a] * 4 + ys[b], "tensor": t}

    def tensor_at(index):
        return {"expert": e, "tensor": index}

    def block(d, k):
        return xs[d] + cores[k]

    sibling = tensor_at(block(0, 1))
    up = tensor_at(block(1, 0))
    down = tensor_at(block(3, 0))
    others = [tensor_at(lax.rem(t + k, 8)) for k in range(1, 8)]

    def remote(src, dst, ssem, rsem, device):
        return pltpu.make_async_remote_copy(
            src_ref=src, dst_ref=dst, send_sem=ssem, recv_sem=rsem,
            device_id=device, device_id_type=MESH,
        )

    def code_copies(l):
        return [
            pltpu.make_async_copy(gc_hbm.at[l], cg, code_sem.at[0]),
            pltpu.make_async_copy(uc_hbm.at[l], cu, code_sem.at[1]),
            pltpu.make_async_copy(dc_hbm.at[l], cd, code_sem.at[2]),
        ]

    barrier = pltpu.get_barrier_semaphore()
    for a in range(4):
        for b in range(4):
            if a or b:
                pl.semaphore_signal(
                    barrier, inc=1, device_id=expert_at(a, b), device_id_type=MESH
                )
    for other in others:
        pl.semaphore_signal(barrier, inc=1, device_id=other, device_id_type=MESH)

    for copy in code_copies(0):
        copy.start()
    eye = (iota((TOK, TOK), 0) == iota((TOK, TOK), 1)).astype(F32)
    stream[...] = tok_ref[...].astype(F32)

    def exchange_copies(l):
        return [
            remote(ex.at[l, 0], ex.at[l, k], ex_s.at[l], ex_r.at[l], others[k - 1])
            for k in range(1, 8)
        ]

    def all_of_exchange(l):
        seven = ex.at[l, pl.ds(1, 7)]
        return remote(seven, seven, ex_s.at[l], ex_r.at[l], sibling)

    def as_row(column):
        return jnp.sum(eye * column, axis=0, keepdims=True)

    def as_column(row):
        return jnp.sum(eye * row, axis=1, keepdims=True)

    below = (iota((TOK, TOK), 0) > iota((TOK, TOK), 1)).astype(BF16)
    lanes = iota((TOK, 16), 1)
    picks, rels = [], []
    for k in range(2):
        named = jnp.sum(
            eye * routes_ref[k : k + 1, :].astype(F32), axis=1, keepdims=True
        ).astype(I32)
        picks.append((named == lanes).astype(F32))
        to_z, to_y = named >> 2, named & 3
        rels.append(((to_z + to_y) & 1) * 8 + to_z * 2 + (to_y >> 1))
    earlier = dot(below, (picks[0] + picks[1]).astype(BF16))
    slots = []
    for k in range(2):
        rank = jnp.sum(picks[k] * earlier, axis=1, keepdims=True)
        slots.append(rels[k].astype(F32) * CAP + rank)
    slot_rows = [as_row(s).astype(I32) for s in slots]
    slot_cols = [s.astype(I32) for s in slots]
    sign = picks[0] - picks[1]

    row = iota((ROWS, 1), 0)
    chunk = row // CHUNK
    inner = row - chunk * CHUNK
    row_half = (inner >= CAP).astype(I32)
    row_slot = chunk * CAP + inner - row_half * CAP
    col_half = (iota((1, 2 * TOK), 1) >= TOK).astype(I32)
    both = [jnp.concatenate([s, s], axis=1) for s in slot_rows]
    hit = (row_half == col_half) & ((row_slot == both[0]) | (row_slot == both[1]))
    gath[...] = hit.astype(F32).astype(BF16)

    @pl.loop(0, 32)
    def _(i):
        at = pl.multiple_of(i * 32, 32)
        r = iota((32, WIDTH), 0) + at
        j = iota((32, WIDTH), 1)
        v = r & (2 * (j & (HALF - 1)) + (j >> 9))
        v = v ^ (v >> 8)
        v = v ^ (v >> 4)
        v = v ^ (v >> 2)
        v = v ^ (v >> 1)
        had[pl.ds(at, 32), :] = (1 - 2 * (v & 1)).astype(F32).astype(BF16)

    def prepare_in(l, step):
        at = pl.multiple_of(step * 32, 32)
        for kind, (codes, scales) in enumerate(((cg, gs_ref), (cu, us_ref))):
            words = [codes[pl.ds(m * HALF + at, 32), :] for m in range(8)]
            shifts = [10 - scales[l, pl.ds(m * 8 + step // 2, 1), :] for m in range(8)]
            for k in range(2):
                values = walsh(
                    ((((w >> (4 * k)) & 15) - 8) << s) for w, s in zip(words, shifts)
                )
                column = k * 256 + kind * 128
                for n in range(8):
                    wp[n, pl.ds(at, 32), column : column + 128] = (
                        values[n].astype(F32).astype(BF16)
                    )

    def prepare_out(l, n):
        for h in range(2):
            at = pl.multiple_of(n * WIDTH + h * HALF, HALF)
            words = cd[:, pl.ds(at, HALF)]
            shift = 8 - ds_ref[l, :, pl.ds(at, HALF)]
            for k in range(2):
                value = (((words >> (4 * k)) & 15) - 8) << shift
                wd[n, pl.ds(h * 128 + k * 64, 64), :] = (
                    value.astype(F32) * (2.0**-8)
                ).astype(BF16)

    def multiply_in(l, s, d, k, first=False):
        n = block(d, k)

        @pl.loop(0, 2)
        def _(i):
            at = pl.ds(pl.multiple_of(i * GROUP, GROUP), GROUP)
            rows = pl.ds(pl.multiple_of((2 * s + i) * GROUP, GROUP), GROUP)
            value = dot(xf[l, d, k, rows, :], wp[n])
            if first:
                acc[at, :] = value
            else:
                acc[at, :] += value

    def multiply_out(s, d, k):
        n = block(d, k)
        target = own if k == 0 else pk1

        @pl.loop(2 * s, 2 * s + 2)
        def _(g):
            at = pl.ds(pl.multiple_of(g * GROUP, GROUP), GROUP)
            target[d, at, :] = dot(actp[at, :], wd[n]).astype(BF16)

    def add_into(d, rows, parts):
        total = own[d, rows, :].astype(F32)
        for part in parts:
            total = total + part[rows, :].astype(F32)
        own[d, rows, :] = total.astype(BF16)

    mix = (
        (iota((256, 256), 0) >> 7 == iota((256, 256), 1) >> 7)
        & (
            iota((256, 256), 1) & 127
            == ((iota((256, 256), 0) & 127) >> 1) + 64 * (iota((256, 256), 0) & 1)
        )
    ).astype(F32).astype(BF16)

    hops = sorted(
        ((a, b) for a in range(4) for b in range(4) if a or b),
        key=lambda ab: -(min(ab[0], 4 - ab[0]) + min(ab[1], 4 - ab[1])),
    )
    targets = [(expert_at(a, b), place(zs[a], ys[b])) for a, b in hops]
    rest = pl.ds(CHUNK, ROWS - CHUNK)

    def dispatch_sent(l):
        remote(
            sl.at[rest, :], xf.at[l, 0, 0, rest, :], disp_s.at[l], disp_r.at[l, 0], sibling
        ).wait_send()

    def slot_values(l):
        gained = (stream[...] * gain_ref[pl.ds(l, 1), :]).astype(BF16)
        for h in range(2):
            xr[pl.ds(h * TOK, TOK), :] = dot(
                gained, had[:, h * HALF : (h + 1) * HALF]
            ).astype(BF16)

        @pl.loop(0, 4)
        def _(p):
            at = pl.ds(pl.multiple_of(p * GROUP, GROUP), GROUP)
            sl[at, :] = dot(gath[at, :], xr[...]).astype(BF16)

        return gained

    def send_slots(l, gained):
        group = lax.div(mine, 4)
        for device, index in targets:
            remote(
                sl.at[chunk_at(index), :], xf.at[l, 0, 0, chunk_at(mine), :],
                disp_s.at[l], disp_r.at[l, group], device,
            ).start()
        pltpu.make_async_copy(
            sl.at[chunk_at(mine), :], xf.at[l, 0, 0, chunk_at(mine), :], disp_r.at[l, group]
        ).start()
        st = stream[...]
        squares = jnp.sum(st * st, axis=1, keepdims=True)
        logits = lax.dot_general(
            gained, rw_ref[l], (((1,), (1,)), ((), ())), preferred_element_type=F32
        )
        diff = jnp.sum(logits * sign, axis=1, keepdims=True)
        ex[l, 0] = jnp.where(iota((8, TOK), 0) == 0, as_row(squares), as_row(diff))
        for copy in exchange_copies(l):
            copy.start()

    def send_scales(l):
        all_of_exchange(l).wait_recv()
        total = ex[l, 0]
        for k in range(1, 8):
            total = total + ex[l, k]
        factor = lax.rsqrt(as_column(total[0:1, :]) / (8 * WIDTH) + 1e-05)
        weights[...] = 1.0 / (1.0 + jnp.exp(-factor * as_column(total[1:2, :])))
        at = iota((TOK, TOK), 1)
        for p in range(4):
            slot = (p * 4 + (at >> 5)) * CAP + (at & 31)
            hit = ((slot == slot_cols[0]) | (slot == slot_cols[1])) & ((at & 31) < CAP)
            row = jnp.sum(jnp.where(hit, factor, 0.0), axis=0, keepdims=True)
            scale_out[l, p] = jnp.broadcast_to(row, (8, TOK))
        for device, index in targets:
            remote(
                scale_out.at[l, lax.div(index, 4)], scales.at[l, mine], scale_s.at[l],
                scale_r.at[l, parity], device,
            ).start()
        pltpu.make_async_copy(
            scale_out.at[l, lax.div(mine, 4)], scales.at[l, mine], scale_r.at[l, parity]
        ).start()

    def combine(l):
        weight = weights[...]
        pltpu.make_async_copy(own.at[0], ret.at[l], ret_r.at[l]).wait()
        for h in range(2):
            part = pl.ds(h * TOK, TOK)
            first = dot(pick[0, part, :], ret[l])
            second = dot(pick[1, part, :], ret[l])
            columns = slice(h * HALF, (h + 1) * HALF)
            stream[:, columns] = (
                stream[:, columns] + weight * first + (1.0 - weight) * second
            )

    def prepare(l):
        codes = code_copies(l)
        for copy in codes:
            copy.wait()

        @pl.loop(0, 16)
        def _(step):
            prepare_in(l, step)

        @pl.loop(0, 8)
        def _(n):
            prepare_out(l, n)

        @pl.when(l + 1 < LAYERS)
        def _():
            for copy in code_copies(l + 1):
                copy.start()

    def gather(l, kind, part, rows, src, dst, device):
        return remote(
            xf.at[(l,) + src + (rows,)], xf.at[(l,) + dst + (rows,)],
            ag_s.at[l, kind], ag_r.at[l, kind, part], device,
        )

    def up_copy(l, g):
        return gather(l, 1, g, rows_of(g), (0, 0), (3, 0), up)

    def down_copy(l, g):
        return gather(l, 2, g, rows_of(g), (0, 0), (1, 0), down)

    def two_copy(l, g):
        if g % 2 == 0:
            return gather(l, 5, g, rows_of(g), (3, 0), (2, 0), up)
        return gather(l, 6, g, rows_of(g), (1, 0), (2, 0), down)

    def two_sib_copy(l, g):
        return gather(l, 7 + g % 2, g, rows_of(g), (2, 0), (2, 1), sibling)

    def sib_copy(l, s, kind, d):
        return gather(l, kind, s, rows_of(2 * s, 2), (d, 0), (d, 1), sibling)

    def send_own(l, s):
        even, odd = 2 * s, 2 * s + 1
        for g in (even, odd):
            arrived = xf.at[l, 0, 0, rows_of(g), :]
            pltpu.make_async_copy(arrived, arrived, disp_r.at[l, g]).wait()
        up_copy(l, even).start()
        down_copy(l, odd).start()
        up_copy(l, odd).start()
        down_copy(l, even).start()
        sib_copy(l, s, 0, 0).start()

    def forward(l, s):
        even, odd = 2 * s, 2 * s + 1
        up_copy(l, even).wait_recv()
        two_copy(l, even).start()
        down_copy(l, odd).wait_recv()
        two_copy(l, odd).start()
        up_copy(l, odd).wait_recv()
        sib_copy(l, s, 3, 3).start()
        down_copy(l, even).wait_recv()
        sib_copy(l, s, 4, 1).start()

    factor = 2.0**-10 / math.sqrt(8 * WIDTH)

    def hidden(l, s):
        even, odd = 2 * s, 2 * s + 1
        multiply_in(l, s, 0, 0, first=True)
        sib_copy(l, s, 0, 0).wait_recv()
        multiply_in(l, s, 0, 1)
        multiply_in(l, s, 3, 0)
        multiply_in(l, s, 1, 0)
        sib_copy(l, s, 3, 3).wait_recv()
        multiply_in(l, s, 3, 1)
        sib_copy(l, s, 4, 1).wait_recv()
        multiply_in(l, s, 1, 1)
        for g in (even, odd):
            two_copy(l, g).wait_recv()
            two_sib_copy(l, g).start()
        multiply_in(l, s, 2, 0)
        for g in (even, odd):
            two_sib_copy(l, g).wait_recv()
        multiply_in(l, s, 2, 1)

        eight = scales.at[l, pl.ds(8 * s, 8)]
        pltpu.make_async_copy(eight, eight, scale_r.at[l, s]).wait()
        lanes_of = iota((CAP, TOK), 1) == iota((CAP, TOK), 0) + lax.rem(mine, 4) * 32

        zero = jnp.zeros((CAP, 128), F32)

        @pl.loop(0, 8)
        def _(j):
            first = pl.ds(pl.multiple_of(j * CHUNK, 8), CAP)
            second = pl.ds(pl.multiple_of(j * CHUNK + CAP, 8), CAP)
            scale = jnp.sum(
                jnp.where(lanes_of, scales[l, 8 * s + j, 0:1, :], 0.0), axis=1, keepdims=True
            )
            total = (acc[first, 0:256] + acc[second, 256:512]) * (factor * scale)
            gate, value = total[:, 0:128], total[:, 128:256]
            act = gate / (1.0 + jnp.exp(-gate)) * value
            actx[first, 0:128] = act
            actx[first, 128:256] = zero
            actx[second, 0:128] = zero
            actx[second, 128:256] = act

        actp[rows_of(2 * s, 2), :] = dot(actx[...].astype(BF16), mix).astype(BF16)

    def sum_sib(l, s, d):
        rows = rows_of(2 * s, 2)
        return remote(
            pk1.at[d, rows, :], sibr.at[l, d, rows, :], rs_s.at[l, 0],
            rs_r.at[l, 0, 4 * s + d], sibling,
        )

    def sum_half(l, g):
        kind = 1 + g % 2
        return remote(
            own.at[2, rows_of(g), :], rh.at[l, rows_of(g), :], rs_s.at[l, kind],
            rs_r.at[l, kind, g], (up, down)[g % 2],
        )

    def sum_owner(l, d, g):
        kind = 3 if d == 1 else 4
        return remote(
            own.at[d, rows_of(g), :], rf.at[l, kind - 3, rows_of(g), :], rs_s.at[l, kind],
            rs_r.at[l, kind, g], up if d == 1 else down,
        )

    def to_sibling(l, s, d):
        multiply_out(s, d, 1)
        sum_sib(l, s, d).start()

    def to_owner(l, d, g, parts):
        add_into(d, rows_of(g), [sibr.at[l, d]] + parts)
        sum_owner(l, d, g).start()

    def sums_start(l, s):
        to_sibling(l, s, 2)
        multiply_out(s, 2, 0)
        to_sibling(l, s, 1)

    def sums_send(l, s):
        even, odd = 2 * s, 2 * s + 1
        sum_sib(l, s, 2).wait_recv()
        for g in (even, odd):
            add_into(2, rows_of(g), [sibr.at[l, 2]])
            sum_half(l, g).start()
        multiply_out(s, 1, 0)
        to_sibling(l, s, 3)
        sum_sib(l, s, 1).wait_recv()
        to_owner(l, 1, odd, [])
        multiply_out(s, 3, 0)
        sum_sib(l, s, 3).wait_recv()
        to_owner(l, 3, even, [])
        to_sibling(l, s, 0)
        multiply_out(s, 0, 0)

    def sums_pass(l, s):
        even, odd = 2 * s, 2 * s + 1
        sum_half(l, even).wait_recv()
        to_owner(l, 1, even, [rh.at[l]])
        sum_half(l, odd).wait_recv()
        to_owner(l, 3, odd, [rh.at[l]])

    def give_back(l, s):
        sum_sib(l, s, 0).wait_recv()
        for g in (2 * s, 2 * s + 1):
            sum_owner(l, 1, g).wait_recv()
            sum_owner(l, 3, g).wait_recv()
            add_into(0, rows_of(g), [sibr.at[l, 0], rf.at[l, 0], rf.at[l, 1]])
            for q in range(4):
                to_z = 2 * (g % 2) + q // 2
                to_y = 2 * (q % 2) + (s + to_z) % 2
                src = own.at[0, pl.ds((g * 4 + q) * CHUNK, CHUNK), :]
                dst = ret.at[l, chunk_at(mine), :]
                here = e == to_z * 4 + to_y

                @pl.when(here)
                def _():
                    pltpu.make_async_copy(src, dst, ret_r.at[l]).start()

                @pl.when(jnp.logical_not(here))
                def _():
                    remote(
                        src, dst, ret_s.at[l], ret_r.at[l],
                        {"expert": to_z * 4 + to_y, "tensor": t},
                    ).start()

    def all_sent(l):
        all_of_exchange(l).wait_send()
        fifteen = scales.at[l, pl.ds(0, 15)]
        remote(fifteen, fifteen, scale_s.at[l], scale_r.at[l, 0], sibling).wait_send()
        for kind in range(9):
            rows = pl.ds(0, ROWS if kind < 5 else PART)
            gather(l, kind, 0, rows, (0, 0), (0, 0), sibling).wait_send()
        remote(pk1, sibr.at[l], rs_s.at[l, 0], rs_r.at[l, 0, 0], sibling).wait_send()
        for kind in range(1, 5):
            rows = pl.ds(0, PART if kind < 3 else ROWS)
            remote(
                own.at[1, rows, :], rh.at[l, rows, :], rs_s.at[l, kind], rs_r.at[l, kind, 0],
                sibling,
            ).wait_send()
        remote(
            own.at[0, rest, :], ret.at[l, rest, :], ret_s.at[l], ret_r.at[l], sibling
        ).wait_send()

    def finish(l):
        combine(l)

        @pl.when(l + 1 < LAYERS)
        def _():
            dispatch_sent(l)
            send_slots(l + 1, slot_values(l + 1))

    def layer(l, carry):
        @pl.when((l > 0) & (parity == 0))
        def _():
            send_scales(l)

        send_own(l, 0)

        @pl.when((l > 0) & (parity == 1))
        def _():
            finish(l - 1)

        @pl.when(l == 0)
        def _():
            send_own(0, 1)
            send_scales(0)
            prepare(0)

        forward(l, 0)

        @pl.when((l > 0) & (parity == 1))
        def _():
            send_scales(l)

        @pl.when(l > 0)
        def _():
            send_own(l, 1)

        hidden(l, 0)

        @pl.when(l > 0)
        def _():
            all_sent(l - 1)

        sums_start(l, 0)
        forward(l, 1)
        sums_send(l, 0)
        hidden(l, 1)
        sums_start(l, 1)
        sums_pass(l, 0)
        sums_send(l, 1)

        @pl.when(l + 1 < LAYERS)
        def _():
            prepare(l + 1)

        give_back(l, 0)
        sums_pass(l, 1)

        @pl.when(parity == 0)
        def _():
            finish(l)

        give_back(l, 1)
        return carry

    gained = slot_values(0)
    pl.semaphore_wait(barrier, 22)
    send_slots(0, gained)
    lane = iota((1, ROWS), 1)
    lane_chunk = lane // CHUNK
    lane_inner = lane - lane_chunk * CHUNK
    lane_half = (lane_inner >= CAP).astype(I32)
    lane_slot = lane_chunk * CAP + lane_inner - lane_half * CAP
    for k in range(2):
        for h in range(2):
            hit = (lane_half == h) & (lane_slot == slot_cols[k])
            pick[k, pl.ds(h * TOK, TOK), :] = hit.astype(F32).astype(BF16)

    lax.fori_loop(0, LAYERS, layer, 0)

    @pl.when(parity == 1)
    def _():
        combine(LAYERS - 1)

    dispatch_sent(LAYERS - 1)
    all_sent(LAYERS - 1)
    out_ref[...] = stream[...].astype(BF16)


def per_device(
    tokens, routes, norm_gain, router_weight, gate_codes, gate_scales, up_codes, up_scales,
    down_codes, down_scales,
):
    vmem = pl.BlockSpec(memory_space=pltpu.VMEM)
    anywhere = pl.BlockSpec(memory_space=pl.ANY)
    dma = pltpu.SemaphoreType.DMA
    return pl.pallas_call(
        kernel,
        out_shape=jax.ShapeDtypeStruct((TOK, WIDTH), BF16),
        in_specs=[
            vmem, vmem, vmem, vmem, anywhere, vmem, anywhere, vmem, anywhere, vmem,
        ],
        out_specs=vmem,
        scratch_shapes=[
            pltpu.VMEM((TOK, WIDTH), F32),
            pltpu.VMEM((WIDTH, WIDTH), BF16),
            pltpu.VMEM((4096, 128), I32),
            pltpu.VMEM((4096, 128), I32),
            pltpu.VMEM((64, 8192), I32),
            pltpu.VMEM((8, HALF, HALF), BF16),
            pltpu.VMEM((8, 256, HALF), BF16),
            pltpu.VMEM((ROWS, 2 * TOK), BF16),
            pltpu.VMEM((2, 2 * TOK, ROWS), BF16),
            pltpu.VMEM((2 * TOK, HALF), BF16),
            pltpu.VMEM((ROWS, HALF), BF16),
            pltpu.VMEM((LAYERS, 4, 2, ROWS, HALF), BF16),
            pltpu.VMEM((PART, HALF), F32),
            pltpu.VMEM((PART, 256), F32),
            pltpu.VMEM((ROWS, 256), BF16),
            pltpu.VMEM((4, ROWS, HALF), BF16),
            pltpu.VMEM((4, ROWS, HALF), BF16),
            pltpu.VMEM((LAYERS, 4, ROWS, HALF), BF16),
            pltpu.VMEM((LAYERS, ROWS, HALF), BF16),
            pltpu.VMEM((LAYERS, 2, ROWS, HALF), BF16),
            pltpu.VMEM((LAYERS, ROWS, HALF), BF16),
            pltpu.VMEM((LAYERS, 8, 8, TOK), F32),
            pltpu.VMEM((TOK, 1), F32),
            pltpu.VMEM((LAYERS, 4, 8, TOK), F32),
            pltpu.VMEM((LAYERS, 16, 8, TOK), F32),
            dma((3,)),
            dma((LAYERS,)), dma((LAYERS,)),
            dma((LAYERS,)), dma((LAYERS, 2)),
            dma((LAYERS,)), dma((LAYERS, 4)),
            dma((LAYERS, 9)), dma((LAYERS, 9, 4)),
            dma((LAYERS, 5)), dma((LAYERS, 5, 8)),
            dma((LAYERS,)), dma((LAYERS,)),
        ],
        compiler_params=pltpu.CompilerParams(
            collective_id=0, has_side_effects=True, vmem_limit_bytes=60 << 20
        ),
        name="moe_layers",
    )(
        tokens, routes.T, norm_gain, router_weight.transpose(0, 2, 1),
        gate_codes.reshape(LAYERS, 4096, 128),
        gate_scales.reshape(LAYERS, 64, 128), up_codes.reshape(LAYERS, 4096, 128),
        up_scales.reshape(LAYERS, 64, 128), down_codes.reshape(LAYERS, 64, 8192),
        down_scales.reshape(LAYERS, 1, 8192),
    )


def solution(mesh):
    in_specs = (
        P("expert", "tensor"),
        P("expert", None),
        P(None, "tensor"),
        P(None, "tensor", None),
        P(None, "expert", None, "tensor"),
        P(None, "expert", None, "tensor"),
        P(None, "expert", None, "tensor"),
        P(None, "expert", None, "tensor"),
        P(None, "expert", "tensor", None),
        P(None, "expert", "tensor", None),
    )
    return jax.shard_map(
        per_device, mesh=mesh, in_specs=in_specs, out_specs=P("expert", "tensor"),
        check_vma=False,
    )
```

time: 183 us -> 160 us (0.87); the launches traced: 180 us -> 160 us
  Pallas kernels: 174 us -> 158 us
  local copies, waits for them, and re-layouts: 6.43 us -> 1.67 us
    pallas_call x1, Pallas kernels: 174 us -> 158 us  [per_device(): pl.pallas_call(kernel, out_shape=jax.ShapeDtypeStruct((TOK, WIDTH), BF16)...]
    unnamed x4 -> x1, local copies, waits for them, and re-layouts: 6.43 us -> 1.67 us
where the time goes in v2:
time: 160 us
  Pallas kernels  158 us (99%)
  local copies, waits for them, and re-layouts  1.67 us (1%)
    pallas_call x1, Pallas kernels, per_device(): pl.pallas_call(kernel, out_shape=jax.ShapeDtypeStruct((TOK, WIDTH), BF16)...  158 us

profile of v2, /device:TPU:9, one launch (start us, length us, event | category | flops | bytes accessed | tf_op | source)
XLA Modules:
  0.0 159.7 jit_solution(891810572912427302)
XLA Ops:
  0.0 158.0 %moe_layers.1 = bf16[128,1024]{1,0:T(8,128)(2,1)} custom-call(bf16[128,1024]{1,0:T(8,128)(2,1)} %tok_ref.1, s32[2,128]{1,0:T(2,128)} %bitcast.15, f32[2,1024]{1,0:T(2,128)} %gain_ref.1, bf16[2,16,1024]{2,1,0:T(8,128)(2,1)} %bitcast.11, s32[2,4096,128]{2,1,0:T(8,128)} %bitcast.8, s32[2,64,128]{2,1,0:T(8,128)} %bitcast.12, s32[2,4096,128]{2,1,0:T(8,128)} %bitcast.9, ...), custom_call_target="tpu_custom_call" | custom-call | tf_op jit(solution)/shard_map/moe_layers/pallas_call | solution.py:615
  158.0 1.7 %copy.12 = bf16[128,1024]{1,0:T(8,128)(2,1)} copy(bf16[128,1024]{1,0:T(8,128)(2,1)} %moe_layers.1) | data formatting | bytes 524288

commit v3 on v2

--- a/solution.py
+++ b/solution.py
@@ -57,8 +57,8 @@
     tok_ref, routes_ref, gain_ref, rw_ref, gc_hbm, gs_ref, uc_hbm, us_ref, dc_hbm, ds_ref,
     out_ref,
     stream, had, cg, cu, cd, wp, wd, gath, pick, xr, sl, xf, acc, actx, actp,
-    own, pk1, sibr, rh, rf, ret, ex, weights, scale_out, scales,
-    code_sem, ex_s, ex_r, scale_s, scale_r, disp_s, disp_r, ag_s, ag_r, rs_s, rs_r, ret_s, ret_r,
+    own, pk1, sibr, rf, ret, far_xr, far_sl, far_sum, far_in, ex, weights, scale_out, scales,
+    code_sem, ex_s, ex_r, scale_s, scale_r, disp_s, disp_r, ag_s, ag_r, rs_s, rs_r, ret_s, ret_r, relay_s, relay_r,
 ):
     e = lax.axis_index("expert")
     t = lax.axis_index("tensor")
@@ -83,6 +83,7 @@
     sibling = tensor_at(block(0, 1))
     up = tensor_at(block(1, 0))
     down = tensor_at(block(3, 0))
+    across = tensor_at(block(2, 0))
     others = [tensor_at(lax.rem(t + k, 8)) for k in range(1, 8)]
 
     def remote(src, dst, ssem, rsem, device):
@@ -239,9 +240,18 @@
     targets = [(expert_at(a, b), place(zs[a], ys[b])) for a, b in hops]
     rest = pl.ds(CHUNK, ROWS - CHUNK)
 
+    def relay(l, step, src, dst):
+        return remote(src, dst, relay_s.at[l, step], relay_r.at[l, step], across)
+
     def dispatch_sent(l):
+        relay(l, 0, xr, far_xr.at[l]).wait_send()
         remote(
-            sl.at[rest, :], xf.at[l, 0, 0, rest, :], disp_s.at[l], disp_r.at[l, 0], sibling
+            far_sl.at[rest, :], xf.at[l, 2, 0, rest, :], disp_s.at[l, 1], disp_r.at[l, 1, 0],
+            sibling,
+        ).wait_send()
+        remote(
+            sl.at[rest, :], xf.at[l, 0, 0, rest, :], disp_s.at[l, 0], disp_r.at[l, 0, 0],
+            sibling,
         ).wait_send()
 
     def slot_values(l):
@@ -258,16 +268,31 @@
 
         return gained
 
-    def send_slots(l, gained):
-        group = lax.div(mine, 4)
+    def to_experts(l, d, rows):
+        which = 0 if d == 0 else 1
         for device, index in targets:
             remote(
-                sl.at[chunk_at(index), :], xf.at[l, 0, 0, chunk_at(mine), :],
-                disp_s.at[l], disp_r.at[l, group], device,
+                rows.at[chunk_at(index), :], xf.at[l, d, 0, chunk_at(mine), :],
+                disp_s.at[l, which], disp_r.at[l, which, parity], device,
             ).start()
         pltpu.make_async_copy(
-            sl.at[chunk_at(mine), :], xf.at[l, 0, 0, chunk_at(mine), :], disp_r.at[l, group]
+            rows.at[chunk_at(mine), :], xf.at[l, d, 0, chunk_at(mine), :],
+            disp_r.at[l, which, parity],
         ).start()
+
+    def relay_slots(l):
+        relay(l, 0, xr, far_xr.at[l]).wait_recv()
+
+        @pl.loop(0, 4)
+        def _(p):
+            at = pl.ds(pl.multiple_of(p * GROUP, GROUP), GROUP)
+            far_sl[at, :] = dot(gath[at, :], far_xr[l]).astype(BF16)
+
+        to_experts(l, 2, far_sl)
+
+    def send_slots(l, gained):
+        relay(l, 0, xr, far_xr.at[l]).start()
+        to_experts(l, 0, sl)
         st = stream[...]
         squares = jnp.sum(st * st, axis=1, keepdims=True)
         logits = lax.dot_general(
@@ -302,15 +327,26 @@
 
     def combine(l):
         weight = weights[...]
-        pltpu.make_async_copy(own.at[0], ret.at[l], ret_r.at[l]).wait()
+        pltpu.make_async_copy(own.at[0], ret.at[l, 0], ret_r.at[l, 0]).wait()
+        relay(l, 1, far_sum, far_in.at[l]).wait_recv()
         for h in range(2):
             part = pl.ds(h * TOK, TOK)
-            first = dot(pick[0, part, :], ret[l])
-            second = dot(pick[1, part, :], ret[l])
+            first = dot(pick[0, part, :], ret[l, 0])
+            second = dot(pick[1, part, :], ret[l, 0])
             columns = slice(h * HALF, (h + 1) * HALF)
             stream[:, columns] = (
                 stream[:, columns] + weight * first + (1.0 - weight) * second
-            )
+            ) + far_in[l, part, :].astype(F32)
+
+    def relay_combine(l):
+        weight = weights[...]
+        pltpu.make_async_copy(own.at[2], ret.at[l, 1], ret_r.at[l, 1]).wait()
+        for h in range(2):
+            part = pl.ds(h * TOK, TOK)
+            first = dot(pick[0, part, :], ret[l, 1])
+            second = dot(pick[1, part, :], ret[l, 1])
+            far_sum[part, :] = (weight * first + (1.0 - weight) * second).astype(BF16)
+        relay(l, 1, far_sum, far_in.at[l]).start()
 
     def prepare(l):
         codes = code_copies(l)
@@ -330,71 +366,52 @@
             for copy in code_copies(l + 1):
                 copy.start()
 
-    def gather(l, kind, part, rows, src, dst, device):
+    def gather(l, s, kind, src, dst, device):
+        rows = rows_of(2 * s, 2)
         return remote(
             xf.at[(l,) + src + (rows,)], xf.at[(l,) + dst + (rows,)],
-            ag_s.at[l, kind], ag_r.at[l, kind, part], device,
+            ag_s.at[l, kind], ag_r.at[l, kind, s], device,
         )
 
-    def up_copy(l, g):
-        return gather(l, 1, g, rows_of(g), (0, 0), (3, 0), up)
-
-    def down_copy(l, g):
-        return gather(l, 2, g, rows_of(g), (0, 0), (1, 0), down)
-
-    def two_copy(l, g):
-        if g % 2 == 0:
-            return gather(l, 5, g, rows_of(g), (3, 0), (2, 0), up)
-        return gather(l, 6, g, rows_of(g), (1, 0), (2, 0), down)
-
-    def two_sib_copy(l, g):
-        return gather(l, 7 + g % 2, g, rows_of(g), (2, 0), (2, 1), sibling)
-
-    def sib_copy(l, s, kind, d):
-        return gather(l, kind, s, rows_of(2 * s, 2), (d, 0), (d, 1), sibling)
+    def up_copy(l, s):
+        return gather(l, s, 1, (0, 0), (3, 0), up)
+
+    def down_copy(l, s):
+        return gather(l, s, 2, (0, 0), (1, 0), down)
+
+    def sib_copy(l, s, d):
+        return gather(l, s, {0: 0, 3: 3, 1: 4, 2: 5}[d], (d, 0), (d, 1), sibling)
+
+    def dispatched(l, s, d):
+        arrived = xf.at[l, d, 0, rows_of(2 * s, 2), :]
+        pltpu.make_async_copy(arrived, arrived, disp_r.at[l, d // 2, s]).wait()
 
     def send_own(l, s):
-        even, odd = 2 * s, 2 * s + 1
-        for g in (even, odd):
-            arrived = xf.at[l, 0, 0, rows_of(g), :]
-            pltpu.make_async_copy(arrived, arrived, disp_r.at[l, g]).wait()
-        up_copy(l, even).start()
-        down_copy(l, odd).start()
-        up_copy(l, odd).start()
-        down_copy(l, even).start()
-        sib_copy(l, s, 0, 0).start()
-
-    def forward(l, s):
-        even, odd = 2 * s, 2 * s + 1
-        up_copy(l, even).wait_recv()
-        two_copy(l, even).start()
-        down_copy(l, odd).wait_recv()
-        two_copy(l, odd).start()
-        up_copy(l, odd).wait_recv()
-        sib_copy(l, s, 3, 3).start()
-        down_copy(l, even).wait_recv()
-        sib_copy(l, s, 4, 1).start()
+        dispatched(l, s, 0)
+        up_copy(l, s).start()
+        down_copy(l, s).start()
+        sib_copy(l, s, 0).start()
 
     factor = 2.0**-10 / math.sqrt(8 * WIDTH)
 
+    def hidden_own(l, s):
+        multiply_in(l, s, 0, 0, first=True)
+        sib_copy(l, s, 0).wait_recv()
+        multiply_in(l, s, 0, 1)
+
     def hidden(l, s):
-        even, odd = 2 * s, 2 * s + 1
-        multiply_in(l, s, 0, 0, first=True)
-        sib_copy(l, s, 0, 0).wait_recv()
-        multiply_in(l, s, 0, 1)
+        dispatched(l, s, 2)
+        sib_copy(l, s, 2).start()
+        multiply_in(l, s, 2, 0)
+        up_copy(l, s).wait_recv()
+        sib_copy(l, s, 3).start()
+        down_copy(l, s).wait_recv()
+        sib_copy(l, s, 1).start()
         multiply_in(l, s, 3, 0)
         multiply_in(l, s, 1, 0)
-        sib_copy(l, s, 3, 3).wait_recv()
-        multiply_in(l, s, 3, 1)
-        sib_copy(l, s, 4, 1).wait_recv()
-        multiply_in(l, s, 1, 1)
-        for g in (even, odd):
-            two_copy(l, g).wait_recv()
-            two_sib_copy(l, g).start()
-        multiply_in(l, s, 2, 0)
-        for g in (even, odd):
-            two_sib_copy(l, g).wait_recv()
-        multiply_in(l, s, 2, 1)
+        for d in (2, 3, 1):
+            sib_copy(l, s, d).wait_recv()
+            multiply_in(l, s, d, 1)
 
         eight = scales.at[l, pl.ds(8 * s, 8)]
         pltpu.make_async_copy(eight, eight, scale_r.at[l, s]).wait()
@@ -426,97 +443,87 @@
             rs_r.at[l, 0, 4 * s + d], sibling,
         )
 
-    def sum_half(l, g):
-        kind = 1 + g % 2
+    def sum_owner(l, s, d):
+        kind = 1 if d == 1 else 2
+        rows = rows_of(2 * s, 2)
         return remote(
-            own.at[2, rows_of(g), :], rh.at[l, rows_of(g), :], rs_s.at[l, kind],
-            rs_r.at[l, kind, g], (up, down)[g % 2],
-        )
-
-    def sum_owner(l, d, g):
-        kind = 3 if d == 1 else 4
-        return remote(
-            own.at[d, rows_of(g), :], rf.at[l, kind - 3, rows_of(g), :], rs_s.at[l, kind],
-            rs_r.at[l, kind, g], up if d == 1 else down,
+            own.at[d, rows, :], rf.at[l, kind - 1, rows, :], rs_s.at[l, kind],
+            rs_r.at[l, kind, s], up if d == 1 else down,
         )
 
     def to_sibling(l, s, d):
         multiply_out(s, d, 1)
         sum_sib(l, s, d).start()
 
-    def to_owner(l, d, g, parts):
-        add_into(d, rows_of(g), [sibr.at[l, d]] + parts)
-        sum_owner(l, d, g).start()
-
-    def sums_start(l, s):
-        to_sibling(l, s, 2)
-        multiply_out(s, 2, 0)
+    def chip_sum(l, s, d):
+        sum_sib(l, s, d).wait_recv()
+        for g in (2 * s, 2 * s + 1):
+            add_into(d, rows_of(g), [sibr.at[l, d]])
+
+    def to_homes(l, g, d):
+        which = 0 if d == 0 else 1
+        for q in range(4):
+            to_z = 2 * (g % 2) + q // 2
+            to_y = 2 * (q % 2) + (g // 2 + to_z) % 2
+            src = own.at[d, pl.ds((g * 4 + q) * CHUNK, CHUNK), :]
+            dst = ret.at[l, which, chunk_at(mine), :]
+            here = e == to_z * 4 + to_y
+
+            @pl.when(here)
+            def _():
+                pltpu.make_async_copy(src, dst, ret_r.at[l, which]).start()
+
+            @pl.when(jnp.logical_not(here))
+            def _():
+                remote(
+                    src, dst, ret_s.at[l, which], ret_r.at[l, which],
+                    {"expert": to_z * 4 + to_y, "tensor": t},
+                ).start()
+
+    def sums(l, s):
         to_sibling(l, s, 1)
-
-    def sums_send(l, s):
-        even, odd = 2 * s, 2 * s + 1
-        sum_sib(l, s, 2).wait_recv()
-        for g in (even, odd):
-            add_into(2, rows_of(g), [sibr.at[l, 2]])
-            sum_half(l, g).start()
         multiply_out(s, 1, 0)
         to_sibling(l, s, 3)
-        sum_sib(l, s, 1).wait_recv()
-        to_owner(l, 1, odd, [])
+        chip_sum(l, s, 1)
+        sum_owner(l, s, 1).start()
         multiply_out(s, 3, 0)
-        sum_sib(l, s, 3).wait_recv()
-        to_owner(l, 3, even, [])
+        to_sibling(l, s, 2)
+        chip_sum(l, s, 3)
+        sum_owner(l, s, 3).start()
+        multiply_out(s, 2, 0)
         to_sibling(l, s, 0)
+        chip_sum(l, s, 2)
+        to_homes(l, 2 * s, 2)
+        to_homes(l, 2 * s + 1, 2)
         multiply_out(s, 0, 0)
-
-    def sums_pass(l, s):
-        even, odd = 2 * s, 2 * s + 1
-        sum_half(l, even).wait_recv()
-        to_owner(l, 1, even, [rh.at[l]])
-        sum_half(l, odd).wait_recv()
-        to_owner(l, 3, odd, [rh.at[l]])
 
     def give_back(l, s):
         sum_sib(l, s, 0).wait_recv()
+        sum_owner(l, s, 1).wait_recv()
+        sum_owner(l, s, 3).wait_recv()
         for g in (2 * s, 2 * s + 1):
-            sum_owner(l, 1, g).wait_recv()
-            sum_owner(l, 3, g).wait_recv()
             add_into(0, rows_of(g), [sibr.at[l, 0], rf.at[l, 0], rf.at[l, 1]])
-            for q in range(4):
-                to_z = 2 * (g % 2) + q // 2
-                to_y = 2 * (q % 2) + (s + to_z) % 2
-                src = own.at[0, pl.ds((g * 4 + q) * CHUNK, CHUNK), :]
-                dst = ret.at[l, chunk_at(mine), :]
-                here = e == to_z * 4 + to_y
-
-                @pl.when(here)
-                def _():
-                    pltpu.make_async_copy(src, dst, ret_r.at[l]).start()
-
-                @pl.when(jnp.logical_not(here))
-                def _():
-                    remote(
-                        src, dst, ret_s.at[l], ret_r.at[l],
-                        {"expert": to_z * 4 + to_y, "tensor": t},
-                    ).start()
+            to_homes(l, g, 0)
 
     def all_sent(l):
         all_of_exchange(l).wait_send()
         fifteen = scales.at[l, pl.ds(0, 15)]
         remote(fifteen, fifteen, scale_s.at[l], scale_r.at[l, 0], sibling).wait_send()
-        for kind in range(9):
-            rows = pl.ds(0, ROWS if kind < 5 else PART)
-            gather(l, kind, 0, rows, (0, 0), (0, 0), sibling).wait_send()
+        for kind in range(6):
+            remote(
+                xf.at[l, 0, 0], xf.at[l, 0, 1], ag_s.at[l, kind], ag_r.at[l, kind, 0], sibling
+            ).wait_send()
         remote(pk1, sibr.at[l], rs_s.at[l, 0], rs_r.at[l, 0, 0], sibling).wait_send()
-        for kind in range(1, 5):
-            rows = pl.ds(0, PART if kind < 3 else ROWS)
+        for kind in range(1, 3):
             remote(
-                own.at[1, rows, :], rh.at[l, rows, :], rs_s.at[l, kind], rs_r.at[l, kind, 0],
-                sibling,
+                own.at[1], rf.at[l, 0], rs_s.at[l, kind], rs_r.at[l, kind, 0], sibling
             ).wait_send()
-        remote(
-            own.at[0, rest, :], ret.at[l, rest, :], ret_s.at[l], ret_r.at[l], sibling
-        ).wait_send()
+        for which in range(2):
+            remote(
+                own.at[0, rest, :], ret.at[l, which, rest, :], ret_s.at[l, which],
+                ret_r.at[l, which], sibling,
+            ).wait_send()
+        relay(l, 1, far_sum, far_in.at[l]).wait_send()
 
     def finish(l):
         combine(l)
@@ -529,6 +536,7 @@
     def layer(l, carry):
         @pl.when((l > 0) & (parity == 0))
         def _():
+            relay_slots(l)
             send_scales(l)
 
         send_own(l, 0)
@@ -537,53 +545,65 @@
         def _():
             finish(l - 1)
 
+        hidden_own(l, 0)
+
         @pl.when(l == 0)
         def _():
+            relay_slots(0)
+            send_scales(0)
             send_own(0, 1)
-            send_scales(0)
-            prepare(0)
-
-        forward(l, 0)
 
         @pl.when((l > 0) & (parity == 1))
         def _():
+            relay_slots(l)
             send_scales(l)
 
+        hidden(l, 0)
+
         @pl.when(l > 0)
         def _():
+            all_sent(l - 1)
             send_own(l, 1)
 
-        hidden(l, 0)
-
-        @pl.when(l > 0)
-        def _():
-            all_sent(l - 1)
-
-        sums_start(l, 0)
-        forward(l, 1)
-        sums_send(l, 0)
+        sums(l, 0)
+        hidden_own(l, 1)
         hidden(l, 1)
-        sums_start(l, 1)
-        sums_pass(l, 0)
-        sums_send(l, 1)
+        sums(l, 1)
 
         @pl.when(l + 1 < LAYERS)
         def _():
             prepare(l + 1)
 
+        @pl.when(parity == 0)
+        def _():
+            relay_combine(l)
+
         give_back(l, 0)
-        sums_pass(l, 1)
 
         @pl.when(parity == 0)
         def _():
             finish(l)
+
+        @pl.when(parity == 1)
+        def _():
+            relay_combine(l)
 
         give_back(l, 1)
         return carry
 
     gained = slot_values(0)
     pl.semaphore_wait(barrier, 22)
+
+    @pl.when(parity == 1)
+    def _():
+        prepare(0)
+
     send_slots(0, gained)
+
+    @pl.when(parity == 0)
+    def _():
+        prepare(0)
+
     lane = iota((1, ROWS), 1)
     lane_chunk = lane // CHUNK
     lane_inner = lane - lane_chunk * CHUNK
@@ -638,9 +658,12 @@
             pltpu.VMEM((4, ROWS, HALF), BF16),
             pltpu.VMEM((4, ROWS, HALF), BF16),
             pltpu.VMEM((LAYERS, 4, ROWS, HALF), BF16),
-            pltpu.VMEM((LAYERS, ROWS, HALF), BF16),
             pltpu.VMEM((LAYERS, 2, ROWS, HALF), BF16),
-            pltpu.VMEM((LAYERS, ROWS, HALF), BF16),
+            pltpu.VMEM((LAYERS, 2, ROWS, HALF), BF16),
+            pltpu.VMEM((LAYERS, 2 * TOK, HALF), BF16),
+            pltpu.VMEM((ROWS, HALF), BF16),
+            pltpu.VMEM((2 * TOK, HALF), BF16),
+            pltpu.VMEM((LAYERS, 2 * TOK, HALF), BF16),
             pltpu.VMEM((LAYERS, 8, 8, TOK), F32),
             pltpu.VMEM((TOK, 1), F32),
             pltpu.VMEM((LAYERS, 4, 8, TOK), F32),
@@ -648,10 +671,11 @@
             dma((3,)),
             dma((LAYERS,)), dma((LAYERS,)),
             dma((LAYERS,)), dma((LAYERS, 2)),
-            dma((LAYERS,)), dma((LAYERS, 4)),
-            dma((LAYERS, 9)), dma((LAYERS, 9, 4)),
-            dma((LAYERS, 5)), dma((LAYERS, 5, 8)),
-            dma((LAYERS,)), dma((LAYERS,)),
+            dma((LAYERS, 2)), dma((LAYERS, 2, 2)),
+            dma((LAYERS, 6)), dma((LAYERS, 6, 2)),
+            dma((LAYERS, 3)), dma((LAYERS, 3, 8)),
+            dma((LAYERS, 2)), dma((LAYERS, 2)),
+            dma((LAYERS, 2)), dma((LAYERS, 2)),
         ],
         compiler_params=pltpu.CompilerParams(
             collective_id=0, has_side_effects=True, vmem_limit_bytes=60 << 20

time: 160 us -> 146 us (0.912)
  Pallas kernels: 158 us -> 142 us
    pallas_call x1, Pallas kernels: 158 us -> 142 us  [per_device(): pl.pallas_call(kernel, out_shape=jax.ShapeDtypeStruct((TOK, WIDTH), BF16)...]
where the time goes in v3:
time: 146 us; the launch traced here: 144 us
  Pallas kernels  142 us (97%)
  local copies, waits for them, and re-layouts  1.67 us (1%)
    pallas_call x1, Pallas kernels, per_device(): pl.pallas_call(kernel, out_shape=jax.ShapeDtypeStruct((TOK, WIDTH), BF16)...  142 us

profile of v3, /device:TPU:9, one launch (start us, length us, event | category | flops | bytes accessed | tf_op | source)
XLA Modules:
  0.0 144.1 jit_solution(6320534527568446724)
XLA Ops:
  0.0 142.4 %moe_layers.1 = bf16[128,1024]{1,0:T(8,128)(2,1)} custom-call(bf16[128,1024]{1,0:T(8,128)(2,1)} %tok_ref.1, s32[2,128]{1,0:T(2,128)} %bitcast.15, f32[2,1024]{1,0:T(2,128)} %gain_ref.1, bf16[2,16,1024]{2,1,0:T(8,128)(2,1)} %bitcast.11, s32[2,4096,128]{2,1,0:T(8,128)} %bitcast.8, s32[2,64,128]{2,1,0:T(8,128)} %bitcast.12, s32[2,4096,128]{2,1,0:T(8,128)} %bitcast.9, ...), custom_call_target="tpu_custom_call" | custom-call | tf_op jit(solution)/shard_map/moe_layers/pallas_call | solution.py:635
  142.4 1.7 %copy.12 = bf16[128,1024]{1,0:T(8,128)(2,1)} copy(bf16[128,1024]{1,0:T(8,128)(2,1)} %moe_layers.1) | data formatting | bytes 524288

commit v4 on v3

--- a/solution.py
+++ b/solution.py
@@ -400,16 +400,16 @@
         multiply_in(l, s, 0, 1)
 
     def hidden(l, s):
-        dispatched(l, s, 2)
-        sib_copy(l, s, 2).start()
-        multiply_in(l, s, 2, 0)
         up_copy(l, s).wait_recv()
         sib_copy(l, s, 3).start()
         down_copy(l, s).wait_recv()
         sib_copy(l, s, 1).start()
         multiply_in(l, s, 3, 0)
         multiply_in(l, s, 1, 0)
-        for d in (2, 3, 1):
+        dispatched(l, s, 2)
+        sib_copy(l, s, 2).start()
+        multiply_in(l, s, 2, 0)
+        for d in (3, 1, 2):
             sib_copy(l, s, d).wait_recv()
             multiply_in(l, s, d, 1)
 
@@ -460,25 +460,29 @@
         for g in (2 * s, 2 * s + 1):
             add_into(d, rows_of(g), [sibr.at[l, d]])
 
-    def to_homes(l, g, d):
+    def to_homes(l, s, d):
         which = 0 if d == 0 else 1
-        for q in range(4):
-            to_z = 2 * (g % 2) + q // 2
-            to_y = 2 * (q % 2) + (g // 2 + to_z) % 2
-            src = own.at[d, pl.ds((g * 4 + q) * CHUNK, CHUNK), :]
+        for i in range(8):
+            low = lax.rem(mine + i, 8)
+            to_z = lax.div(low, 2)
+            to_y = 2 * lax.rem(low, 2) + lax.rem(to_z + s, 2)
+            src = own.at[d, chunk_at(low + 8 * s), :]
             dst = ret.at[l, which, chunk_at(mine), :]
-            here = e == to_z * 4 + to_y
-
-            @pl.when(here)
+            away = remote(
+                src, dst, ret_s.at[l, which], ret_r.at[l, which],
+                {"expert": to_z * 4 + to_y, "tensor": t},
+            )
+            if i:
+                away.start()
+                continue
+
+            @pl.when(parity == s)
             def _():
                 pltpu.make_async_copy(src, dst, ret_r.at[l, which]).start()
 
-            @pl.when(jnp.logical_not(here))
+            @pl.when(parity != s)
             def _():
-                remote(
-                    src, dst, ret_s.at[l, which], ret_r.at[l, which],
-                    {"expert": to_z * 4 + to_y, "tensor": t},
-                ).start()
+                away.start()
 
     def sums(l, s):
         to_sibling(l, s, 1)
@@ -493,8 +497,7 @@
         multiply_out(s, 2, 0)
         to_sibling(l, s, 0)
         chip_sum(l, s, 2)
-        to_homes(l, 2 * s, 2)
-        to_homes(l, 2 * s + 1, 2)
+        to_homes(l, s, 2)
         multiply_out(s, 0, 0)
 
     def give_back(l, s):
@@ -503,7 +506,7 @@
         sum_owner(l, s, 3).wait_recv()
         for g in (2 * s, 2 * s + 1):
             add_into(0, rows_of(g), [sibr.at[l, 0], rf.at[l, 0], rf.at[l, 1]])
-            to_homes(l, g, 0)
+        to_homes(l, s, 0)
 
     def all_sent(l):
         all_of_exchange(l).wait_send()
@@ -539,12 +542,11 @@
             relay_slots(l)
             send_scales(l)
 
+        @pl.when((l > 0) & (parity == 1))
+        def _():
+            finish(l - 1)
+
         send_own(l, 0)
-
-        @pl.when((l > 0) & (parity == 1))
-        def _():
-            finish(l - 1)
-
         hidden_own(l, 0)
 
         @pl.when(l == 0)
@@ -558,12 +560,15 @@
             relay_slots(l)
             send_scales(l)
 
+        @pl.when(l > 0)
+        def _():
+            send_own(l, 1)
+
         hidden(l, 0)
 
         @pl.when(l > 0)
         def _():
             all_sent(l - 1)
-            send_own(l, 1)
 
         sums(l, 0)
         hidden_own(l, 1)
@@ -580,15 +585,16 @@
 
         give_back(l, 0)
 
+        @pl.when(parity == 1)
+        def _():
+            relay_combine(l)
+
+        give_back(l, 1)
+
         @pl.when(parity == 0)
         def _():
             finish(l)
 
-        @pl.when(parity == 1)
-        def _():
-            relay_combine(l)
-
-        give_back(l, 1)
         return carry
 
     gained = slot_values(0)

time: 146 us -> 139 us (0.952)
  the two profiles are of different devices: /device:TPU:9 before, /device:TPU:34 now
where the time goes in v4:
time: 139 us
  Pallas kernels  137 us (99%)
  local copies, waits for them, and re-layouts  1.67 us (1%)
    pallas_call x1, Pallas kernels, per_device(): pl.pallas_call(kernel, out_shape=jax.ShapeDtypeStruct((TOK, WIDTH), BF16)...  137 us

profile of v4, /device:TPU:34, one launch (start us, length us, event | category | flops | bytes accessed | tf_op | source)
XLA Modules:
  0.0 138.8 jit_solution(5324055833963030185)
XLA Ops:
  0.0 137.1 %moe_layers.1 = bf16[128,1024]{1,0:T(8,128)(2,1)} custom-call(bf16[128,1024]{1,0:T(8,128)(2,1)} %tok_ref.1, s32[2,128]{1,0:T(2,128)} %bitcast.15, f32[2,1024]{1,0:T(2,128)} %gain_ref.1, bf16[2,16,1024]{2,1,0:T(8,128)(2,1)} %bitcast.11, s32[2,4096,128]{2,1,0:T(8,128)} %bitcast.8, s32[2,64,128]{2,1,0:T(8,128)} %bitcast.12, s32[2,4096,128]{2,1,0:T(8,128)} %bitcast.9, ...), custom_call_target="tpu_custom_call" | custom-call | tf_op jit(solution)/shard_map/moe_layers/pallas_call | solution.py:641
  137.1 1.7 %copy.12 = bf16[128,1024]{1,0:T(8,128)(2,1)} copy(bf16[128,1024]{1,0:T(8,128)(2,1)} %moe_layers.1) | data formatting | bytes 524288

commit v5 on v4

--- a/solution.py
+++ b/solution.py
@@ -198,26 +198,16 @@
                 ).astype(BF16)
 
     def multiply_in(l, s, d, k, first=False):
-        n = block(d, k)
-
-        @pl.loop(0, 2)
-        def _(i):
-            at = pl.ds(pl.multiple_of(i * GROUP, GROUP), GROUP)
-            rows = pl.ds(pl.multiple_of((2 * s + i) * GROUP, GROUP), GROUP)
-            value = dot(xf[l, d, k, rows, :], wp[n])
-            if first:
-                acc[at, :] = value
-            else:
-                acc[at, :] += value
+        value = dot(xf[l, d, k, rows_of(2 * s, 2), :], wp[block(d, k)])
+        if first:
+            acc[...] = value
+        else:
+            acc[...] += value
 
     def multiply_out(s, d, k):
-        n = block(d, k)
         target = own if k == 0 else pk1
-
-        @pl.loop(2 * s, 2 * s + 2)
-        def _(g):
-            at = pl.ds(pl.multiple_of(g * GROUP, GROUP), GROUP)
-            target[d, at, :] = dot(actp[at, :], wd[n]).astype(BF16)
+        rows = rows_of(2 * s, 2)
+        target[d, rows, :] = dot(actp[rows, :], wd[block(d, k)]).astype(BF16)
 
     def add_into(d, rows, parts):
         total = own[d, rows, :].astype(F32)
@@ -254,18 +244,16 @@
             sibling,
         ).wait_send()
 
-    def slot_values(l):
+    def slot_values(l, ready):
         gained = (stream[...] * gain_ref[pl.ds(l, 1), :]).astype(BF16)
         for h in range(2):
             xr[pl.ds(h * TOK, TOK), :] = dot(
                 gained, had[:, h * HALF : (h + 1) * HALF]
             ).astype(BF16)
 
-        @pl.loop(0, 4)
-        def _(p):
-            at = pl.ds(pl.multiple_of(p * GROUP, GROUP), GROUP)
-            sl[at, :] = dot(gath[at, :], xr[...]).astype(BF16)
-
+        if ready:
+            relay(l, 0, xr, far_xr.at[l]).start()
+        sl[...] = dot(gath[...], xr[...]).astype(BF16)
         return gained
 
     def to_experts(l, d, rows):
@@ -282,16 +270,10 @@
 
     def relay_slots(l):
         relay(l, 0, xr, far_xr.at[l]).wait_recv()
-
-        @pl.loop(0, 4)
-        def _(p):
-            at = pl.ds(pl.multiple_of(p * GROUP, GROUP), GROUP)
-            far_sl[at, :] = dot(gath[at, :], far_xr[l]).astype(BF16)
-
+        far_sl[...] = dot(gath[...], far_xr[l]).astype(BF16)
         to_experts(l, 2, far_sl)
 
     def send_slots(l, gained):
-        relay(l, 0, xr, far_xr.at[l]).start()
         to_experts(l, 0, sl)
         st = stream[...]
         squares = jnp.sum(st * st, axis=1, keepdims=True)
@@ -419,10 +401,9 @@
 
         zero = jnp.zeros((CAP, 128), F32)
 
-        @pl.loop(0, 8)
-        def _(j):
-            first = pl.ds(pl.multiple_of(j * CHUNK, 8), CAP)
-            second = pl.ds(pl.multiple_of(j * CHUNK + CAP, 8), CAP)
+        for j in range(8):
+            first = pl.ds(j * CHUNK, CAP)
+            second = pl.ds(j * CHUNK + CAP, CAP)
             scale = jnp.sum(
                 jnp.where(lanes_of, scales[l, 8 * s + j, 0:1, :], 0.0), axis=1, keepdims=True
             )
@@ -486,14 +467,14 @@
 
     def sums(l, s):
         to_sibling(l, s, 1)
+        to_sibling(l, s, 3)
         multiply_out(s, 1, 0)
-        to_sibling(l, s, 3)
         chip_sum(l, s, 1)
         sum_owner(l, s, 1).start()
         multiply_out(s, 3, 0)
-        to_sibling(l, s, 2)
         chip_sum(l, s, 3)
         sum_owner(l, s, 3).start()
+        to_sibling(l, s, 2)
         multiply_out(s, 2, 0)
         to_sibling(l, s, 0)
         chip_sum(l, s, 2)
@@ -534,7 +515,7 @@
         @pl.when(l + 1 < LAYERS)
         def _():
             dispatch_sent(l)
-            send_slots(l + 1, slot_values(l + 1))
+            send_slots(l + 1, slot_values(l + 1, True))
 
     def layer(l, carry):
         @pl.when((l > 0) & (parity == 0))
@@ -575,30 +556,31 @@
         hidden(l, 1)
         sums(l, 1)
 
+        @pl.when(parity == 0)
+        def _():
+            relay_combine(l)
+
+        give_back(l, 0)
+
+        @pl.when(parity == 1)
+        def _():
+            relay_combine(l)
+
+        give_back(l, 1)
+
         @pl.when(l + 1 < LAYERS)
         def _():
             prepare(l + 1)
 
         @pl.when(parity == 0)
         def _():
-            relay_combine(l)
-
-        give_back(l, 0)
-
-        @pl.when(parity == 1)
-        def _():
-            relay_combine(l)
-
-        give_back(l, 1)
-
-        @pl.when(parity == 0)
-        def _():
             finish(l)
 
         return carry
 
-    gained = slot_values(0)
+    gained = slot_values(0, False)
     pl.semaphore_wait(barrier, 22)
+    relay(0, 0, xr, far_xr.at[0]).start()
 
     @pl.when(parity == 1)
     def _():

time: 139 us -> 128 us (0.921)
  the two profiles are of different devices: /device:TPU:34 before, /device:TPU:9 now
where the time goes in v5:
time: 128 us; the launch traced here: 127 us
  Pallas kernels  125 us (98%)
  local copies, waits for them, and re-layouts  1.67 us (1%)
    pallas_call x1, Pallas kernels, per_device(): pl.pallas_call(kernel, out_shape=jax.ShapeDtypeStruct((TOK, WIDTH), BF16)...  125 us

profile of v5, /device:TPU:9, one launch (start us, length us, event | category | flops | bytes accessed | tf_op | source)
XLA Modules:
  0.0 126.6 jit_solution(22648499222238626)
XLA Ops:
  0.0 125.0 %moe_layers.1 = bf16[128,1024]{1,0:T(8,128)(2,1)} custom-call(bf16[128,1024]{1,0:T(8,128)(2,1)} %tok_ref.1, s32[2,128]{1,0:T(2,128)} %bitcast.15, f32[2,1024]{1,0:T(2,128)} %gain_ref.1, bf16[2,16,1024]{2,1,0:T(8,128)(2,1)} %bitcast.11, s32[2,4096,128]{2,1,0:T(8,128)} %bitcast.8, s32[2,64,128]{2,1,0:T(8,128)} %bitcast.12, s32[2,4096,128]{2,1,0:T(8,128)} %bitcast.9, ...), custom_call_target="tpu_custom_call" | custom-call | tf_op jit(solution)/shard_map/moe_layers/pallas_call | solution.py:623
  125.0 1.7 %copy.12 = bf16[128,1024]{1,0:T(8,128)(2,1)} copy(bf16[128,1024]{1,0:T(8,128)(2,1)} %moe_layers.1) | data formatting | bytes 524288

commit v6 on v5

--- a/solution.py
+++ b/solution.py
@@ -246,10 +246,9 @@
 
     def slot_values(l, ready):
         gained = (stream[...] * gain_ref[pl.ds(l, 1), :]).astype(BF16)
+        turned = dot(gained, had[...]).astype(BF16)
         for h in range(2):
-            xr[pl.ds(h * TOK, TOK), :] = dot(
-                gained, had[:, h * HALF : (h + 1) * HALF]
-            ).astype(BF16)
+            xr[pl.ds(h * TOK, TOK), :] = turned[:, h * HALF : (h + 1) * HALF]
 
         if ready:
             relay(l, 0, xr, far_xr.at[l]).start()
@@ -310,11 +309,12 @@
     def combine(l):
         weight = weights[...]
         pltpu.make_async_copy(own.at[0], ret.at[l, 0], ret_r.at[l, 0]).wait()
+        picked = dot(pick[...], ret[l, 0])
         relay(l, 1, far_sum, far_in.at[l]).wait_recv()
         for h in range(2):
             part = pl.ds(h * TOK, TOK)
-            first = dot(pick[0, part, :], ret[l, 0])
-            second = dot(pick[1, part, :], ret[l, 0])
+            first = picked[h * TOK : (h + 1) * TOK]
+            second = picked[(2 + h) * TOK : (3 + h) * TOK]
             columns = slice(h * HALF, (h + 1) * HALF)
             stream[:, columns] = (
                 stream[:, columns] + weight * first + (1.0 - weight) * second
@@ -323,10 +323,11 @@
     def relay_combine(l):
         weight = weights[...]
         pltpu.make_async_copy(own.at[2], ret.at[l, 1], ret_r.at[l, 1]).wait()
+        picked = dot(pick[...], ret[l, 1])
         for h in range(2):
             part = pl.ds(h * TOK, TOK)
-            first = dot(pick[0, part, :], ret[l, 1])
-            second = dot(pick[1, part, :], ret[l, 1])
+            first = picked[h * TOK : (h + 1) * TOK]
+            second = picked[(2 + h) * TOK : (3 + h) * TOK]
             far_sum[part, :] = (weight * first + (1.0 - weight) * second).astype(BF16)
         relay(l, 1, far_sum, far_in.at[l]).start()
 
@@ -600,7 +601,7 @@
     for k in range(2):
         for h in range(2):
             hit = (lane_half == h) & (lane_slot == slot_cols[k])
-            pick[k, pl.ds(h * TOK, TOK), :] = hit.astype(F32).astype(BF16)
+            pick[pl.ds((2 * k + h) * TOK, TOK), :] = hit.astype(F32).astype(BF16)
 
     lax.fori_loop(0, LAYERS, layer, 0)
 
@@ -636,7 +637,7 @@
             pltpu.VMEM((8, HALF, HALF), BF16),
             pltpu.VMEM((8, 256, HALF), BF16),
             pltpu.VMEM((ROWS, 2 * TOK), BF16),
-            pltpu.VMEM((2, 2 * TOK, ROWS), BF16),
+            pltpu.VMEM((4 * TOK, ROWS), BF16),
             pltpu.VMEM((2 * TOK, HALF), BF16),
             pltpu.VMEM((ROWS, HALF), BF16),
             pltpu.VMEM((LAYERS, 4, 2, ROWS, HALF), BF16),

time: 128 us -> 128 us (level)
  no operation moved by 1% of the time
where the time goes in v6:
time: 128 us; the launch traced here: 127 us
  Pallas kernels  125 us (98%)
  local copies, waits for them, and re-layouts  1.67 us (1%)
    pallas_call x1, Pallas kernels, per_device(): pl.pallas_call(kernel, out_shape=jax.ShapeDtypeStruct((TOK, WIDTH), BF16)...  125 us

profile of v6, /device:TPU:9, one launch (start us, length us, event | category | flops | bytes accessed | tf_op | source)
XLA Modules:
  0.0 127.0 jit_solution(5289903336058377636)
XLA Ops:
  0.0 125.4 %moe_layers.1 = bf16[128,1024]{1,0:T(8,128)(2,1)} custom-call(bf16[128,1024]{1,0:T(8,128)(2,1)} %tok_ref.1, s32[2,128]{1,0:T(2,128)} %bitcast.15, f32[2,1024]{1,0:T(2,128)} %gain_ref.1, bf16[2,16,1024]{2,1,0:T(8,128)(2,1)} %bitcast.11, s32[2,4096,128]{2,1,0:T(8,128)} %bitcast.8, s32[2,64,128]{2,1,0:T(8,128)} %bitcast.12, s32[2,4096,128]{2,1,0:T(8,128)} %bitcast.9, ...), custom_call_target="tpu_custom_call" | custom-call | tf_op jit(solution)/shard_map/moe_layers/pallas_call | solution.py:624
  125.4 1.7 %copy.12 = bf16[128,1024]{1,0:T(8,128)(2,1)} copy(bf16[128,1024]{1,0:T(8,128)(2,1)} %moe_layers.1) | data formatting | bytes 524288
